TPU v7x, 256 devices: a whole 4x4x8 slice. The times are simulated.
256 devices in a mesh: mem: 4 (over y_hi, core), reg: 64 (over y_lo, x, z).
Axes of the slice: x: 4, y: 4 (y_hi: 2, y_lo: 2; y = y_hi * 2 + y_lo), z: 8, core: 2. Of those that a mesh axis runs over, the one named last changes fastest.
Arguments:
- prior_samples: bfloat16 [256, 512, 512], P('mem', 'reg'), may hold values from -6 to 6
- measured_sample_anomalies: bfloat16 [16384, 128, 256], P(('mem', 'reg')), may hold values from -4 to 4
- reciprocal_noise_spread: float32 [16384, 128], P(('mem', 'reg')), may hold values from 0.3 to 3
- measured_departure: float32 [16384, 128], P(('mem', 'reg')), may hold values from -6 to 6
- measurement_tally: int32 [16384], P(('mem', 'reg')), may hold values from 32 to 128
- group_destination_zone: int32 [16384, 1], P(('mem', 'reg')), may hold values from 0 to 63; in each aligned block of 64 rows (0 to 63, 64 to 127, ...) at most 2 rows name the same one
- group_nearby_tile: int32 [16384], P(('mem', 'reg')), may hold values from 0 to 7
Outputs:
- analysis: bfloat16 [256, 512, 512], P('mem', 'reg')
Inputs may be any that keep to these rules, and one draw needn't show every extreme that they name: `measurement_tally`: valid observations of a block stand in its first rows. `group_destination_zone`: at most 2 of the blocks of one device name the same region; in every draw some device has exactly 2 blocks naming one region.
All inputs are finite; a program needn't handle non-finite values.
Results may differ from a plain program's by a relative error of at most 0.0069.
Values may be sent and summed in bfloat16 or wider, within the bound.
No kernel may reach another device: no remote copies, remote signals or barrier semaphores. Data moves between devices by JAX's collectives and lax.ppermute only.
A program may use at most 128 MiB of HBM per device.

v0:
```python
import math

import jax
import jax.numpy as jnp
from jax import lax
from jax.sharding import PartitionSpec as P

SAMPLE_NUMBER = 256
OB = 128
BLK_DEV = 64
PATCH_DEV = 2
ITERS = 5


def in_one_piece(arrays, axis, split_dim, concat_dim, along):
    columns = [a.reshape(*a.shape[:along], -1) for a in arrays]
    both = jnp.concatenate(columns, axis=along)
    whole, at, done = (
        lax.all_to_all(both, axis, split_axis=split_dim, concat_axis=concat_dim, tiled=True),
        0,
        [],
    )
    for a, column in zip(arrays, columns):
        section = whole[..., at : at + column.shape[along]]
        done.append(section.reshape(*section.shape[:along], *a.shape[along:]))
        at += column.shape[along]
    return tuple(done)


def split_up(shard, dim, devices):
    before, after = (shard.shape[:dim], shard.shape[dim + 1 :])
    return jnp.moveaxis(shard.reshape(*before, devices, -1, *after), dim, 0)


def sum_at_owner(shard, axis, dim):
    blocks = split_up(shard, dim, lax.axis_size(axis))
    arrived = lax.all_to_all(blocks, axis, split_axis=0, concat_axis=0, tiled=True)
    return arrived.sum(axis=0)


def in_one_piece_2(arrays, axis, dim, along):
    widths = [math.prod(a.shape[along:]) for a in arrays]
    both = jnp.concatenate(
        [a.reshape(*a.shape[:along], w) for a, w in zip(arrays, widths)], axis=along
    )
    whole = sum_at_owner(both, axis, dim)
    blocks = jnp.split(whole, [sum(widths[:k]) for k in range(1, len(widths))], axis=along)
    return tuple(
        (b.reshape(*whole.shape[:along], *a.shape[along:]) for a, b in zip(arrays, blocks))
    )


def matmul_high(left, right):
    return jnp.matmul(left, right, precision=lax.Precision.HIGHEST)


def weight_matrices(gram_part, drive_part):
    identity = jnp.eye(SAMPLE_NUMBER, dtype=jnp.float32)
    gram_full = gram_part + (SAMPLE_NUMBER - 1.0) * identity
    frob_scale = jnp.sqrt(jnp.sum(gram_full * gram_full, axis=(1, 2)))[:, None, None]
    root_iter = gram_full / frob_scale
    inverse_iter = jnp.broadcast_to(identity, gram_full.shape)
    for sweep in range(ITERS):
        newton_step = 1.5 * identity - 0.5 * matmul_high(inverse_iter, root_iter)
        root_iter = matmul_high(root_iter, newton_step)
        inverse_iter = matmul_high(newton_step, inverse_iter)
    inv_root = inverse_iter / jnp.sqrt(frob_scale)
    mean_weight = matmul_high(inv_root, matmul_high(inv_root, drive_part[:, :, None]))
    return (math.sqrt(SAMPLE_NUMBER - 1.0) * inv_root + mean_weight).astype(jnp.bfloat16)


def patch_totals(rows_all, obs_all, tags_all, patch_region):
    group_count = rows_all.shape[0] // 8
    patch_hot = (
        tags_all.astype(jnp.int32)[:, None] == jnp.arange(patch_region, dtype=jnp.int32)[None, :]
    ).astype(jnp.float32)

    def accumulate(totals, block_item):
        rows_block, obs_block, hot_block = block_item
        block_grams = jnp.einsum(
            "gok,gol->gkl", rows_block, rows_block, preferred_element_type=jnp.float32
        )
        drives = jnp.einsum("gok,go->gk", rows_block, obs_block, preferred_element_type=jnp.float32)
        gram_next = totals[0] + jnp.einsum(
            "gp,gkl->pkl", hot_block, block_grams, precision=lax.Precision.HIGHEST
        )
        drive_next = totals[1] + jnp.einsum(
            "gp,gk->pk", hot_block, drives, precision=lax.Precision.HIGHEST
        )
        return ((gram_next, drive_next), None)

    start_totals = (
        jnp.zeros((patch_region, SAMPLE_NUMBER, SAMPLE_NUMBER), jnp.float32),
        jnp.zeros((patch_region, SAMPLE_NUMBER), jnp.float32),
    )
    (gram_sum, drive_sum), unused = lax.scan(
        accumulate,
        start_totals,
        (
            rows_all.reshape(group_count, 8, OB, SAMPLE_NUMBER),
            obs_all.reshape(group_count, 8, OB),
            patch_hot.reshape(group_count, 8, patch_region),
        ),
    )
    return (gram_sum, drive_sum)


def per_device(
    prior_samples,
    measured_sample_anomalies,
    reciprocal_noise_spread,
    measured_departure,
    measurement_tally,
    group_destination_zone,
    group_nearby_tile,
):
    regions = lax.axis_size("reg")
    members = lax.axis_size("mem")
    capacity = max(2, (2 * BLK_DEV + regions - 1) // regions)
    slot_total = regions * capacity
    patch_region = PATCH_DEV * members
    field_tiles = lax.all_to_all(prior_samples, "mem", split_axis=1, concat_axis=0, tiled=True)
    is_valid = (
        lax.broadcasted_iota(jnp.int32, reciprocal_noise_spread.shape, 1)
        < measurement_tally[:, None]
    )
    row_weight = jnp.where(
        is_valid, reciprocal_noise_spread, jnp.zeros_like(reciprocal_noise_spread)
    )
    scaled = (measured_sample_anomalies * row_weight[:, :, None]).astype(jnp.bfloat16)
    weighted = (measured_departure * row_weight).astype(jnp.bfloat16)
    region_index = group_destination_zone[:, 0]
    region_hot = (region_index[:, None] == jnp.arange(regions, dtype=jnp.int32)[None, :]).astype(
        jnp.int32
    )
    rank_region = jnp.sum(jnp.cumsum(region_hot, axis=0) * region_hot, axis=1) - 1
    slot_index = region_index * capacity + rank_region
    send_rows = jnp.zeros((slot_total, OB, SAMPLE_NUMBER), jnp.bfloat16).at[slot_index].set(scaled)
    send_obs = jnp.zeros((slot_total, OB), jnp.bfloat16).at[slot_index].set(weighted)
    send_tags = (
        jnp.zeros((slot_total,), jnp.bfloat16)
        .at[slot_index]
        .set(group_nearby_tile.astype(jnp.bfloat16))
    )
    recv_rows, recv_obs, recv_tags = in_one_piece((send_rows, send_obs, send_tags), "reg", 0, 0, 1)
    gram_sum, drive_sum = patch_totals(recv_rows, recv_obs, recv_tags, patch_region)
    gram_own, drive_own = in_one_piece_2((gram_sum, drive_sum), "mem", 0, 2)
    weights = weight_matrices(gram_own, drive_own)
    sample_average_field = jnp.sum(field_tiles, axis=0, dtype=jnp.float32) / SAMPLE_NUMBER
    sample_deviation_field = (field_tiles - sample_average_field).astype(jnp.bfloat16)
    update = jnp.einsum(
        "jpx,pjk->kpx", sample_deviation_field, weights, preferred_element_type=jnp.float32
    )
    analysis = (sample_average_field[None] + update).astype(jnp.bfloat16)
    return lax.all_to_all(analysis, "mem", split_axis=0, concat_axis=1, tiled=True)


def solution(mesh):
    placed = (
        P("mem", "reg", None),
        P(("mem", "reg"), None, None),
        P(("mem", "reg"), None),
        P(("mem", "reg"), None),
        P(("mem", "reg")),
        P(("mem", "reg"), None),
        P(("mem", "reg")),
    )
    return jax.shard_map(
        per_device, mesh=mesh, in_specs=placed, out_specs=P("mem", "reg", None), check_vma=False
    )
```

profile of v0, /device:TPU:40, one launch (start us, length us, event | category | flops | bytes accessed | tf_op | source)
XLA Modules:
  0.0 438.8 jit_solution(16043560860479048522)
XLA Ops:
  3.2 4.2 multiply_convert_fusion
  7.4 4.3 broadcast_in_dim.19
  11.6 11.9 %scatter_fusion = bf16[128,128,256]{2,1,0:T(8,128)(2,1)} fusion(bf16[128,128,256]{2,1,0:T(8,128)(2,1)} %broadcast_in_dim.19, s32[64]{0:T(128)S(1)} %fusion.38, bf16[64,128,256]{2,1,0:T(8,128)(2,1)} %multiply_convert_fusion), kind=kCustom, calls=%fused_computation | custom fusion | bytes 12583168 | tf_op jit(solution)/shard_map/scatter | solution.py:138
  23.6 12.6 %concatenate.18 = bf16[64,2,32768]{2,1,0:T(2,128)(2,1)} reshape(bf16[128,128,256]{2,1,0:T(8,128)(2,1)} %scatter_fusion) | data formatting | bytes 16777216 | tf_op jit(solution)/shard_map/concatenate | solution.py:17
  38.2 9.5 %pad_maximum_fusion = bf16[64,2,32897]{2,1,0:T(2,128)(2,1)} fusion(bf16[64,2,1]{2,1,0:T(2,128)(2,1)S(1)} %concatenate.25, bf16[64,2,128]{2,1,0:T(2,128)(2,1)S(1)} %bitcast.93, bf16[64,2,32768]{2,1,0:T(2,128)(2,1)} %concatenate.18), kind=kLoop, calls=%fused_computation.21 | loop fusion | flops 25264896 | bytes 16843264 | tf_op jit(solution)/shard_map/concatenate | solution.py:17
  47.7 12.9 %all-to-all-start.1 = ((bf16[64,2,32897]{2,1,0:T(2,128)(2,1)}), bf16[64,2,32897]{2,1,0:T(2,128)(2,1)}, u32[]{:S(2)}, u32[]{:S(2)}) async-start(bf16[64,2,32897]{2,1,0:T(2,128)(2,1)} %pad_maximum_fusion), calls=%async_computation.1 | async-start | bytes 16908288 | tf_op jit(solution)/shard_map/all_to_all | solution.py:19
  61.6 187.6 %all-to-all-done.1 = bf16[64,2,32897]{2,1,0:T(2,128)(2,1)} async-done(((bf16[64,2,32897]{2,1,0:T(2,128)(2,1)}), bf16[64,2,32897]{2,1,0:T(2,128)(2,1)}, u32[]{:S(2)}, u32[]{:S(2)}) %all-to-all-start.1) | async-done | bytes 8421664 | tf_op jit(solution)/shard_map/all_to_all | solution.py:19
  249.2 4.3 all-to-all-start
  253.5 14.3 %all_to_all.31 = bf16[128,32897]{1,0:T(8,128)(2,1)} reshape(bf16[64,2,32897]{2,1,0:T(2,128)(2,1)} %all-to-all-done.1) | data formatting | bytes 16843264 | tf_op jit(solution)/shard_map/all_to_all | solution.py:19
  267.8 7.3 %slice.13 = bf16[128,32768]{1,0:T(8,128)(2,1)} slice(bf16[128,32897]{1,0:T(8,128)(2,1)} %all_to_all.31), slice={[0:128], [0:32768]} | slice | bytes 16777216 | tf_op jit(solution)/shard_map/slice | solution.py:24
  276.9 93.7 %while.13 = (s32[]{:T(128)}, f32[8,256,256]{2,0,1:T(8,128)S(1)}, f32[8,256]{1,0:T(8,128)S(1)}, f32[16,8,8]{2,1,0:T(8,128)S(1)}, bf16[16,8,128,256]{3,1,2,0:T(8,1...) while((s32[]{:T(128)}, f32[8,256,256]{2,0,1:T(8,128)S(1)}, ...), condition=%wide.region_8.9_spmd.clone, body=%wide.region_7.8_spmd.clone.sunk | while | flops 186322944 | bytes 10532976 | solution.py:96
  278.9 3.8 select_add_fusion.2
  284.8 3.8 select_add_fusion.2
  290.7 3.8 select_add_fusion.2
  296.5 3.8 select_add_fusion.2
  302.4 3.8 select_add_fusion.2
  308.2 3.8 select_add_fusion.2
  314.1 3.8 select_add_fusion.2
  319.9 3.8 select_add_fusion.2
  325.8 3.8 select_add_fusion.2
  331.6 3.8 select_add_fusion.2
  337.5 3.8 select_add_fusion.2
  343.4 3.8 select_add_fusion.2
  349.2 3.8 select_add_fusion.2
  355.1 3.8 select_add_fusion.2
  360.9 3.8 select_add_fusion.2
  366.8 3.8 select_add_fusion.2
  374.5 2.2 pad_maximum_fusion.1
  376.7 2.6 copy.116
  379.2 4.6 %all-to-all-start.2 = ((f32[4,2,256,257]{2,1,3,0:T(2,128)}), f32[4,2,256,257]{2,1,3,0:T(2,128)S(1)}, u32[]{:S(2)}, u32[]{:S(2)}) async-start(f32[4,2,256,257]{2,1,3,0:T(2,128)} %copy.116), calls=%async_computation.2 | async-start | bytes 4210688 | tf_op jit(solution)/shard_map/all_to_all | solution.py:37
  388.7 22.4 %all-to-all-done.2 = f32[4,2,256,257]{2,1,3,0:T(2,128)S(1)} async-done(((f32[4,2,256,257]{2,1,3,0:T(2,128)}), f32[4,2,256,257]{2,1,3,0:T(2,128)S(1)}, u32[]{:S(2)}, u32[]{:S(2)}) %all-to-all-start.2) | async-done | bytes 2105376 | tf_op jit(solution)/shard_map/all_to_all | solution.py:37
  424.7 12.7 %all_to_all.41 = bf16[256,2,512]{2,1,0:T(2,128)(2,1)S(1)} all-to-all(bf16[256,2,512]{2,1,0:T(2,128)(2,1)S(1)} %copy.122), channel_id=1, replica_groups=mesh['mem'=4,'reg'=64] {'mem'}, dimensions={0} | all-to-all | bytes 1048576 | tf_op jit(solution)/shard_map/all_to_all | solution.py:155
  (153 shorter events, 63.0 us)
Async XLA Ops:
  23.5 12.6 %copy-start.7 = (s32[64]{0:T(128)S(1)}, s32[64]{0:T(128)}, u32[]{:S(2)}) copy-start(s32[64]{0:T(128)} %param.15) | copy-start | bytes 772
  23.5 13.8 %copy-start.4 = (f32[64,128]{1,0:T(8,128)S(1)}, f32[64,128]{1,0:T(8,128)}, u32[]{:S(2)}) copy-start(f32[64,128]{1,0:T(8,128)} %param.11) | copy-start | bytes 98308
  23.6 13.8 %copy-start.5 = (f32[64,128]{1,0:T(8,128)S(1)}, f32[64,128]{1,0:T(8,128)}, u32[]{:S(2)}) copy-start(f32[64,128]{1,0:T(8,128)} %param.12) | copy-start | bytes 98308
  23.6 13.8 %copy-start.6 = (s32[64]{0:T(128)S(1)}, s32[64]{0:T(128)}, u32[]{:S(2)}) copy-start(s32[64]{0:T(128)} %param.13) | copy-start | bytes 772
  47.7 12.9 %copy-start.3 = (bf16[64,8,512]{2,1,0:T(8,128)(2,1)S(1)}, bf16[64,8,512]{2,1,0:T(8,128)(2,1)}, u32[]{:S(2)}) copy-start(bf16[64,8,512]{2,1,0:T(8,128)(2,1)} %param.9) | copy-start | bytes 1572868
  47.7 201.4 %all-to-all-start.1 = ((bf16[64,2,32897]{2,1,0:T(2,128)(2,1)}), bf16[64,2,32897]{2,1,0:T(2,128)(2,1)}, u32[]{:S(2)}, u32[]{:S(2)}) async-start(bf16[64,2,32897]{2,1,0:T(2,128)(2,1)} %pad_maximum_fusion), calls=%async_computation.1 | async-start | bytes 16908288 | tf_op jit(solution)/shard_map/all_to_all | solution.py:19
  249.2 130.1 %all-to-all-start = ((bf16[64,8,512]{2,0,1:T(8,128)(2,1)}), bf16[64,8,512]{2,0,1:T(8,128)(2,1)}, u32[]{:S(2)}, u32[]{:S(2)}) async-start(bf16[64,8,512]{2,0,1:T(8,128)(2,1)} %copy.110), calls=%async_computation | async-start | bytes 1048576 | tf_op jit(solution)/shard_map/all_to_all | solution.py:122
  379.2 31.8 %all-to-all-start.2 = ((f32[4,2,256,257]{2,1,3,0:T(2,128)}), f32[4,2,256,257]{2,1,3,0:T(2,128)S(1)}, u32[]{:S(2)}, u32[]{:S(2)}) async-start(f32[4,2,256,257]{2,1,3,0:T(2,128)} %copy.116), calls=%async_computation.2 | async-start | bytes 4210688 | tf_op jit(solution)/shard_map/all_to_all | solution.py:37
  388.7 24.0 %copy-start.2 = (f32[256,256]{1,0:T(8,128)S(1)}, f32[256,256]{1,0:T(8,128)}, u32[]{:S(2)}) copy-start(f32[256,256]{1,0:T(8,128)} %get-tuple-element.117) | copy-start | bytes 786436
  388.7 24.3 %copy-start.1 = (f32[256,256]{1,0:T(8,128)S(1)}, f32[256,256]{1,0:T(8,128)}, u32[]{:S(2)}) copy-start(f32[256,256]{1,0:T(8,128)} %fusion.29) | copy-start | bytes 786436
  419.7 4.0 copy-start
where the time goes:
time: 441 us; the launch traced here: 439 us
  waiting for transfers between devices  210 us (48%)
  matrix products  86.5 us (20%)
  local copies, waits for them, and re-layouts  79.8 us (18%)
  other arithmetic  27 us (6%)
  starting transfers between devices  21.8 us (5%)
  blocking collectives  12.7 us (3%)
    all_to_all x1, waiting for transfers between devices, in_one_piece(): lax.all_to_all(both, axis, split_axis=split_dim, concat_axis=concat_dim,...  188 us
    dot_general x16, matrix products, accumulate(): jnp.einsum('gp,gkl->pkl', hot_block, block_grams, precision=lax.Precision...  61.5 us
    all_to_all x1, waiting for transfers between devices, sum_at_owner(): lax.all_to_all(blocks, axis, split_axis=0, concat_axis=0, tiled=True)  22.4 us
    dynamic_slice x16, local copies, waits for them, and re-layouts, patch_totals(): lax.scan(accumulate, start_totals, (rows_all.reshape(group_count, 8, OB,...  17.3 us
    all_to_all x1, local copies, waits for them, and re-layouts, in_one_piece(): lax.all_to_all(both, axis, split_axis=split_dim, concat_axis=concat_dim,...  14.3 us
    all_to_all x1, starting transfers between devices, in_one_piece(): lax.all_to_all(both, axis, split_axis=split_dim, concat_axis=concat_dim,...  12.9 us
    concatenate x2, local copies, waits for them, and re-layouts, in_one_piece(): both = jnp.concatenate(columns, axis=along)  12.8 us
    all_to_all x1, blocking collectives, per_device(): lax.all_to_all(analysis, 'mem', split_axis=0, concat_axis=1, tiled=True)  12.7 us
  transfers between devices with their start and end apart: 3, of which 2 were waited for; matrix products, arithmetic and copies ran while one was open for 27% of the time, Pallas kernels for 0%

commit v1 on v0

v1 whole, which is shorter than its diff:
```python
import functools
import math

import jax
import jax.numpy as jnp
from jax import lax
from jax.experimental import pallas as pl
from jax.experimental.pallas import tpu as pltpu
from jax.sharding import Mesh
from jax.sharding import PartitionSpec as P

SAMPLE_NUMBER = 256
OB = 128
CAP = 2
PATCH_REG = 8
ITERS = 5
META = 16
ROWS = CAP * OB + META
HALF = SAMPLE_NUMBER // 2
MEMBERS = SAMPLE_NUMBER // 4
PACK = 2 * HALF + 16
GROUP = ("mem", "ylo", "x", "zp")
STEP = 8
TAGS = 16


def prep_kernel(
    ways, zone_smem, tally_smem, tile_smem, anom_ref, spread_ref, depart_ref, out_ref, anom_buf,
    meta_wide, counts, sems
):
    blocks = anom_ref.shape[0]
    regions = out_ref.shape[0]
    zq_ways, plane_ways, zp_ways = ways

    def load(g):
        part = pl.ds(g * STEP, STEP)
        return pltpu.make_async_copy(anom_ref.at[part], anom_buf.at[part], sems.at[g])

    for g in range(blocks // STEP):
        load(g).start()

    @pl.loop(0, regions)
    def _(r):
        counts[r] = 0

    meta_wide[...] = jnp.zeros_like(meta_wide)
    row = lax.broadcasted_iota(jnp.int32, (OB, 1), 0)
    lane = lax.broadcasted_iota(jnp.int32, (1, OB), 1)

    @pl.loop(0, blocks // STEP)
    def _(g):
        part = pl.ds(pl.multiple_of(g * STEP, STEP), STEP)
        spread, depart = spread_ref[part, :], depart_ref[part, :]
        spread_t = spread.T
        load(g).wait()
        for j in range(STEP):
            b = g * STEP + j
            region = zone_smem[b]
            rank = counts[region]
            counts[region] = rank + 1
            rest = region // zp_ways
            place = (rest % zq_ways * plane_ways + rest // zq_ways) * zp_ways + region % zp_ways

            weight = jnp.where(row < tally_smem[b], spread_t[:, j : j + 1], 0.0)
            scaled = anom_buf[b].astype(jnp.float32) * weight
            start = pl.multiple_of(rank * OB, OB)
            out_ref[place, pl.ds(start, OB), :] = scaled.astype(jnp.bfloat16)

            kept = jnp.where(lane < tally_smem[b], spread[j : j + 1], 0.0)
            tag = jnp.full((1, OB), tile_smem[b] + 1, jnp.int32).astype(jnp.float32)
            content = jnp.concatenate([depart[j : j + 1] * kept, tag], axis=1)
            meta_wide[place, pl.ds(rank, 1), :] = content

    out_ref[:, CAP * OB :, :] = meta_wide[...].astype(jnp.bfloat16)


def build_messages(anomalies, spread, departure, tally, tile, zone, ways):
    blocks = anomalies.shape[0]
    regions = math.prod(ways)
    scalars = pl.BlockSpec(memory_space=pltpu.SMEM)
    vectors = pl.BlockSpec(memory_space=pltpu.VMEM)
    return pl.pallas_call(
        functools.partial(prep_kernel, ways),
        out_shape=jax.ShapeDtypeStruct((regions, ROWS, SAMPLE_NUMBER), jnp.bfloat16),
        in_specs=[scalars] * 3 + [pl.BlockSpec(memory_space=pl.ANY)] + [vectors] * 2,
        out_specs=vectors,
        scratch_shapes=[
            pltpu.VMEM((blocks, OB, SAMPLE_NUMBER), jnp.bfloat16),
            pltpu.VMEM((regions, META, SAMPLE_NUMBER), jnp.float32),
            pltpu.SMEM((regions,), jnp.int32),
            pltpu.SemaphoreType.DMA((blocks // STEP,)),
        ],
        compiler_params=pltpu.CompilerParams(vmem_limit_bytes=24 << 20),
        cost_estimate=pl.CostEstimate(flops=0, bytes_accessed=1 << 23, transcendentals=0),
        name="build_messages",
    )(zone, tally, tile, anomalies, spread, departure)


def high_low(row):
    high = row.astype(jnp.bfloat16)
    return high, (row - high.astype(jnp.float32)).astype(jnp.bfloat16)


def gram_kernel(tag_ref, rows_ref, *refs):
    outs, (upper, corner, tag_vmem, tag_smem, tag_sem) = refs[:4], refs[4:]
    step, zq = pl.program_id(0), lax.axis_index("zq")
    sources = rows_ref.shape[0]

    @pl.when(step == 0)
    def _():
        weight = lax.broadcasted_iota(jnp.int32, tag_ref.shape, 1)
        weight = jnp.where(weight == 0, 1.0, jnp.where(weight == 1, TAGS, 0.0))
        codes = jnp.sum(tag_ref[...].astype(jnp.float32) * weight, axis=1)
        tag_vmem[...] = codes.astype(jnp.int32)
        tag_copy = pltpu.make_async_copy(tag_vmem, tag_smem, tag_sem)
        tag_copy.start()
        upper[...] = jnp.zeros_like(upper)
        corner[...] = jnp.zeros_like(corner)
        tag_copy.wait()

    place = lax.broadcasted_iota(jnp.int32, (META, OB), 0)
    for s in range(sources):
        meta = rows_ref[s, CAP * OB : ROWS, :OB].astype(jnp.float32)
        for i in range(CAP):
            code = tag_smem[step * sources + s, 0]
            tag = (code // TAGS if i else code % TAGS) - 1
            turned = (tag // 2 - zq + 4) % 4 * 2 + tag % 2
            tag = jnp.where(tag >= 0, turned, PATCH_REG)
            block = rows_ref[s, i * OB : (i + 1) * OB, :]
            flipped = block.T
            innovation = jnp.where(place == i, meta, 0.0).astype(jnp.bfloat16)
            left = jnp.concatenate([flipped[:HALF], innovation], axis=0)
            upper[tag] += jnp.dot(left, block, preferred_element_type=jnp.float32)
            corner[tag] += jnp.dot(
                flipped[HALF:], block[:, HALF:], preferred_element_type=jnp.float32
            )

    @pl.when(step == pl.num_programs(0) - 1)
    def _():
        row = lax.broadcasted_iota(jnp.int32, (HALF, HALF), 0)
        col = lax.broadcasted_iota(jnp.int32, (HALF, HALF), 1)
        for p in range(PATCH_REG):
            first, last = upper[p, :HALF, :HALF], corner[p]
            mixed = jnp.where(row >= col, first, last)
            diagonal = jnp.sum(jnp.where(row == col, last, 0.0), axis=0, keepdims=True)
            drive = jnp.sum(upper[p, HALF:, :], axis=0, keepdims=True)
            extra = jnp.concatenate([diagonal, drive[:, :HALF], drive[:, HALF:]], axis=0)
            high, low = high_low(extra)
            tail = jnp.concatenate(
                [
                    high.astype(jnp.float32),
                    low.astype(jnp.float32),
                    jnp.zeros((PACK - 2 * HALF - 6, HALF), jnp.float32),
                ],
                axis=0,
            )
            out = outs[p // 2]
            out[p % 2, :HALF, :] = upper[p, :HALF, HALF:].astype(jnp.bfloat16)
            out[p % 2, HALF : 2 * HALF, :] = mixed.astype(jnp.bfloat16)
            out[p % 2, 2 * HALF :, :] = tail.astype(jnp.bfloat16)


def partial_grams(messages):
    regions = messages.shape[0]
    sources = min(8, regions)
    piece = jax.ShapeDtypeStruct((2, PACK, HALF), jnp.bfloat16)
    return pl.pallas_call(
        gram_kernel,
        out_shape=[piece] * 4,
        grid_spec=pl.GridSpec(
            grid=(regions // sources,),
            in_specs=[
                pl.BlockSpec((regions, META, OB), lambda i: (0, CAP * OB // META, 1)),
                pl.BlockSpec((sources, ROWS, SAMPLE_NUMBER), lambda i: (i, 0, 0)),
            ],
            out_specs=[pl.BlockSpec((2, PACK, HALF), lambda i: (0, 0, 0))] * 4,
            scratch_shapes=[
                pltpu.VMEM((PATCH_REG + 1, HALF + META, SAMPLE_NUMBER), jnp.float32),
                pltpu.VMEM((PATCH_REG + 1, HALF, HALF), jnp.float32),
                pltpu.VMEM((regions, OB), jnp.int32),
                pltpu.SMEM((regions, OB), jnp.int32),
                pltpu.SemaphoreType.DMA,
            ],
        ),
        compiler_params=pltpu.CompilerParams(vmem_limit_bytes=12 << 20),
        cost_estimate=pl.CostEstimate(flops=1 << 31, bytes_accessed=1 << 23, transcendentals=0),
        name="partial_grams",
    )(messages, messages)


def split(a):
    high = a.astype(jnp.bfloat16)
    return high, (a - high.astype(jnp.float32)).astype(jnp.bfloat16)


def product(a, b):
    dot = functools.partial(jnp.dot, preferred_element_type=jnp.float32)
    return dot(a[0], b[0]) + (dot(a[0], b[1]) + dot(a[1], b[0]))


def newton_kernel(a_ref, b_ref, c_ref, d_ref, *refs):
    zq = lax.axis_index("zq")
    outs, (gram_ref, weight_ref) = refs[:4], refs[4:]
    row = lax.broadcasted_iota(jnp.int32, (HALF, HALF), 0)
    col = lax.broadcasted_iota(jnp.int32, (HALF, HALF), 1)
    row_full = lax.broadcasted_iota(jnp.int32, (SAMPLE_NUMBER, SAMPLE_NUMBER), 0)
    col_full = lax.broadcasted_iota(jnp.int32, (SAMPLE_NUMBER, SAMPLE_NUMBER), 1)
    identity = jnp.where(row_full == col_full, 1.0, 0.0)
    for p in range(2):
        total = sum(ref[p].astype(jnp.float32) for ref in (a_ref, b_ref, c_ref, d_ref))
        cross, mixed, tail = total[:HALF], total[HALF : 2 * HALF], total[2 * HALF :]
        extra = tail[0:3] + tail[3:6]
        turned = mixed.T
        gram_ref[p, :HALF, :HALF] = jnp.where(row >= col, mixed, turned)
        gram_ref[p, :HALF, HALF:] = cross
        gram_ref[p, HALF:, :HALF] = cross.T
        gram_ref[p, HALF:, HALF:] = jnp.where(
            row == col, extra[0:1], jnp.where(row < col, mixed, turned)
        )
        drive = jnp.concatenate([extra[1:2], extra[2:3]], axis=1)
        gram = gram_ref[p] + (SAMPLE_NUMBER - 1.0) * identity
        squares = jnp.sum(jnp.sum(gram * gram, axis=0, keepdims=True), axis=1, keepdims=True)
        frob = jnp.sqrt(squares)
        root = gram / frob
        inverse = step = 1.5 * identity - 0.5 * root
        for sweep in range(1, ITERS):
            step_parts = split(step)
            root = product(split(root), step_parts)
            inverse_parts = split(inverse)
            step = 1.5 * identity - 0.5 * product(inverse_parts, split(root))
            inverse = product(split(step), inverse_parts)
        inv_root = inverse / jnp.sqrt(frob)
        once = jnp.sum(inv_root * drive, axis=1, keepdims=True)
        mean_weight = jnp.sum(inv_root * once, axis=0, keepdims=True)
        weight_ref[...] = math.sqrt(SAMPLE_NUMBER - 1.0) * inv_root + mean_weight
        for e in range(4):
            goal = (zq + e) % 4
            part = weight_ref[pl.ds(pl.multiple_of(goal * MEMBERS, MEMBERS), MEMBERS), :]
            low, high = part[:, :HALF], part[:, HALF:]
            low, high = jnp.where(goal >= 2, high, low), jnp.where(goal >= 2, low, high)
            for i, side in enumerate((low, high)):
                side = jnp.where(goal % 2 == 1, pltpu.roll(side, MEMBERS, 1), side)
                outs[e][p, :, i * HALF : (i + 1) * HALF] = side.astype(jnp.bfloat16)


def flipped_weights(pieces):
    piece = jax.ShapeDtypeStruct((2, MEMBERS, SAMPLE_NUMBER), jnp.bfloat16)
    return pl.pallas_call(
        newton_kernel,
        out_shape=[piece] * 4,
        scratch_shapes=[
            pltpu.VMEM((2, SAMPLE_NUMBER, SAMPLE_NUMBER), jnp.float32),
            pltpu.VMEM((SAMPLE_NUMBER, SAMPLE_NUMBER), jnp.float32),
        ],
        compiler_params=pltpu.CompilerParams(vmem_limit_bytes=12 << 20),
        name="weights",
    )(*pieces)


def analysis_kernel(perturb_ref, mean_ref, *refs):
    routed, out_ref = refs[:4], refs[4]
    mem = lax.axis_index("mem")
    for e in range(4):
        for i in range(2):
            p = (mem - e + 4) % 4 * 2 + i
            update = jnp.dot(routed[e][i], perturb_ref[p], preferred_element_type=jnp.float32)
            out_ref[p] = (mean_ref[p] + update).astype(jnp.bfloat16)


def analysed(perturb, state_mean, routed):
    return pl.pallas_call(
        analysis_kernel,
        out_shape=jax.ShapeDtypeStruct(
            (PATCH_REG, MEMBERS, perturb.shape[2]), jnp.bfloat16
        ),
        compiler_params=pltpu.CompilerParams(vmem_limit_bytes=12 << 20),
        name="analysed",
    )(perturb, state_mean, *routed)


def shift(x, axis, by):
    n = lax.axis_size(axis)
    return lax.ppermute(x, axis, [(j, (j + by) % n) for j in range(n)])


def swap(x, bit):
    return lax.ppermute(x, "mem", [(j, j ^ bit) for j in range(4)])


def per_device(prior, anomalies, spread, departure, tally, zone, tile):
    ways = {a: lax.axis_size(a) for a in ("ylo", "x", "zq", "zp")}
    in_hbm = lambda x: pltpu.with_memory_space_constraint(x, pltpu.HBM)
    messages = build_messages(
        *(in_hbm(x) for x in (anomalies, spread, departure, tally, tile, zone[:, 0])),
        (ways["zq"], ways["ylo"] * ways["x"], ways["zp"]),
    )
    near, far = swap(prior, 1), swap(prior, 2)
    messages, near, far = lax.optimization_barrier((messages, near, far))
    arrived = lax.all_to_all(messages, GROUP, split_axis=0, concat_axis=0, tiled=True)
    arrived, near, far = lax.optimization_barrier((arrived, near, far))
    farther = swap(far, 1)

    pieces = partial_grams(arrived)
    pieces = [pieces[0]] + [shift(pieces[d], "zq", d) for d in range(1, 4)]

    field = jnp.concatenate([prior, near, far, farther], axis=0).transpose(1, 0, 2)
    state_mean = jnp.sum(field, axis=1, keepdims=True, dtype=jnp.float32) / SAMPLE_NUMBER
    perturb = (field - state_mean).astype(jnp.bfloat16)
    pieces, state_mean, perturb = lax.optimization_barrier((pieces, state_mean, perturb))
    weights = flipped_weights(pieces)

    routed = [
        lax.ppermute(
            weights[e],
            ("mem", "zq"),
            [(m * 4 + z, (z + e) % 4 * 4 + m) for m in range(4) for z in range(4)],
        )
        for e in range(4)
    ]
    return analysed(perturb, state_mean, routed).transpose(1, 0, 2)


def solution(mesh):
    grid = Mesh(mesh.devices.reshape(4, 2, 4, 4, 2), ("mem", "ylo", "x", "zq", "zp"))
    return on_grid(grid)


def on_grid(grid):
    reg = ("ylo", "x", "zq", "zp")
    every = ("mem",) + reg
    placed = (
        P("mem", reg, None),
        P(every, None, None),
        P(every, None),
        P(every, None),
        P(every),
        P(every, None),
        P(every),
    )
    return jax.shard_map(
        per_device, mesh=grid, in_specs=placed, out_specs=P("mem", reg, None), check_vma=False
    )
```

time: 441 us -> 185 us (0.42)
  waiting for transfers between devices: 210 us -> 26.2 us
  blocking collectives: 12.7 us -> 111 us
  matrix products: 86.5 us -> 0 us
  local copies, waits for them, and re-layouts: 79.8 us -> 2.3 us
  other arithmetic: 27 us -> 0.74 us
  Pallas kernels: 0 us -> 18.1 us
    all_to_all x3 -> x0, waiting for transfers between devices: 210 us -> none  [the longest x1 188 us: in_one_piece(): lax.all_to_all(both, axis, split_axis=split_dim, concat_axis=concat_dim,...]
    all_to_all x1, blocking collectives: 12.7 us -> 111 us  [per_device(): lax.all_to_all(messages, GROUP, split_axis=0, concat_axis=0, tiled=True)]
    dot_general x81 -> x0, matrix products: 86.5 us -> none  [the longest x16 61.5 us: accumulate(): jnp.einsum('gp,gkl->pkl', hot_block, block_grams, precision=lax.Precision...]
    ppermute x0 -> x10, waiting for transfers between devices: none -> 26.2 us  [the longest x3 9.7 us: shift(): return lax.ppermute(x, axis, [(j, (j + by) % n) for j in range(n)])]
    ppermute x0 -> x10, starting transfers between devices: none -> 24 us  [the longest x4 11.1 us: per_device(): lax.ppermute(weights[e], ('mem', 'zq'), [(m * 4 + z, (z + e) % 4 * 4 + m)...]
    all_to_all x3 -> x0, starting transfers between devices: 21.8 us -> none  [the longest x1 12.9 us: in_one_piece(): lax.all_to_all(both, axis, split_axis=split_dim, concat_axis=concat_dim,...]
    pallas_call x0 -> x4, Pallas kernels: none -> 18.1 us  [the longest x1 7.28 us: partial_grams(): pl.pallas_call(gram_kernel, out_shape=[piece] * 4, grid_spec=pl.GridSpec(...]
    dynamic_slice x16 -> x0, local copies, waits for them, and re-layouts: 17.3 us -> none  [patch_totals(): lax.scan(accumulate, start_totals, (rows_all.reshape(group_count, 8, OB,...]
  transfers between devices with their start and end apart: 3 -> 10, of which waited for: 2 -> 5; matrix products, arithmetic and copies ran while one was open for 27% -> 0% of each run, Pallas kernels for 0% -> 6%
where the time goes in v1:
time: 185 us; the launch traced here: 183 us
  blocking collectives  111 us (60%)
  waiting for transfers between devices  26.2 us (14%)
  starting transfers between devices  24 us (13%)
  Pallas kernels  18.1 us (10%)
  local copies, waits for them, and re-layouts  2.3 us (1%)
    all_to_all x1, blocking collectives, per_device(): lax.all_to_all(messages, GROUP, split_axis=0, concat_axis=0, tiled=True)  111 us
    ppermute x4, starting transfers between devices, per_device(): lax.ppermute(weights[e], ('mem', 'zq'), [(m * 4 + z, (z + e) % 4 * 4 + m)...  11.1 us
    ppermute x3, starting transfers between devices, shift(): return lax.ppermute(x, axis, [(j, (j + by) % n) for j in range(n)])  10.5 us
    ppermute x3, waiting for transfers between devices, shift(): return lax.ppermute(x, axis, [(j, (j + by) % n) for j in range(n)])  9.7 us
    ppermute x3, waiting for transfers between devices, swap(): return lax.ppermute(x, 'mem', [(j, j ^ bit) for j in range(4)])  8.39 us
    ppermute x4, waiting for transfers between devices, per_device(): lax.ppermute(weights[e], ('mem', 'zq'), [(m * 4 + z, (z + e) % 4 * 4 + m)...  8.1 us
    pallas_call x1, Pallas kernels, partial_grams(): pl.pallas_call(gram_kernel, out_shape=[piece] * 4, grid_spec=pl.GridSpec(...  7.28 us
    pallas_call x1, Pallas kernels, flipped_weights(): pl.pallas_call(newton_kernel, out_shape=[piece] * 4, scratch_shapes=[pltp...  5.84 us
  transfers between devices with their start and end apart: 10, of which 5 were waited for; matrix products, arithmetic and copies ran while one was open for 0% of the time, Pallas kernels for 6%

profile of v1, /device:TPU:40, one launch (start us, length us, event | category | flops | bytes accessed | tf_op | source)
XLA Modules:
  0.0 182.8 jit_solution(4718915580751423022)
XLA Ops:
  0.0 1.2 copy.8
  1.2 2.4 %collective-permute-start.1 = (bf16[64,8,512]{2,0,1:T(8,128)(2,1)S(1)}, bf16[64,8,512]{2,0,1:T(8,128)(2,1)S(1)}, u32[]{:S(2)}, u32[]{:S(2)}) collective-permute-start(bf16[64,8,512]{2,0,1:T(8,128)(2,1)S(1)} %copy.8), channel_id=1, source_target_pairs={{0,128},{64,192},{128,0},{192,64},{1,129},{65,193},{129,1},{193,65... | collective-permute-start | bytes 1572872 | tf_op jit(solution)/shard_map/ppermute | solution.py:287
  3.6 0.0 collective-permute-start
  3.6 4.5 %build_messages.1 = bf16[64,272,256]{2,1,0:T(8,128)(2,1)S(1)} custom-call(s32[64]{0:T(128)} %bitcast.8, s32[64]{0:T(128)} %tally_smem.1, s32[64]{0:T(128)} %tile_smem.1, bf16[64,128,256]{2,1,0:T(8,128)(2,1)} %anom_ref.1, f32[64,128]{1,0:T(8,128)} %spread_ref.1, f32[64,128]{1,0:T(8,128)} %depart_ref.1), custom_call_target="tpu_custom_call" | custom-call | bytes 8388608 | tf_op jit(solution)/shard_map/build_messages/pallas_call | solution.py:82
  8.1 8.4 %collective-permute-done.1 = bf16[64,8,512]{2,0,1:T(8,128)(2,1)S(1)} collective-permute-done((bf16[64,8,512]{2,0,1:T(8,128)(2,1)S(1)}, bf16[64,8,512]{2,0,1:T(8,128)(2,1)S(1)}, u32[]{:S(2)}, u32[]{:S(2)}) %collective-permute-start.1) | collective-permute-done | bytes 524320 | tf_op jit(solution)/shard_map/ppermute | solution.py:287
  16.5 0.0 collective-permute-done
  16.5 111.4 %all_to_all.5.tag_ref.rows_ref = bf16[64,272,256]{2,1,0:T(8,128)(2,1)S(1)} all-to-all(bf16[64,272,256]{2,1,0:T(8,128)(2,1)S(1)} %build_messages.1), channel_id=1, replica_groups=mesh['mem'=4,'ylo'=2,'x'=4,'zq'=4,'zp'=2] {'mem','ylo','x','zp'}, dimensions={0} | all-to-all | bytes 17825792 | tf_op jit(solution)/shard_map/all_to_all | solution.py:299
  127.9 0.0 collective-permute-start.5
  127.9 7.3 %partial_grams.1 = (bf16[2,272,128]{2,1,0:T(8,128)(2,1)S(1)}, bf16[2,272,128]{2,1,0:T(8,128)(2,1)S(1)}, bf16[2,272,128]{2,1,0:T(8,128)(2,1)S(1)}, bf16[2,272,128]{2,1,0:T(8,128)(2,1)S(1)}) custom-call(bf16[64,272,256]{2,1,0:T(8,128)(2,1)S(1)} %all_to_all.5.tag_ref.rows_ref, bf16[64,272,256]{2,1,0:T(8,128)(2,1)S(1)} %all_to_all.5.tag_ref.rows_ref), custom_call_target="tpu_custom_call" | custom-call | flops 2147483648 | bytes 8388608 | tf_op jit(solution)/shard_map/partial_grams/pallas_call | solution.py:167
  135.2 3.4 %collective-permute-start.2 = (bf16[2,272,128]{2,1,0:T(8,128)(2,1)S(1)}, bf16[2,272,128]{2,1,0:T(8,128)(2,1)S(1)}, u32[]{:S(2)}, u32[]{:S(2)}) collective-permute-start(bf16[2,272,128]{2,1,0:T(8,128)(2,1)S(1)} %get-tuple-element.30), channel_id=1, source_target_pairs={{0,2},{2,4},{4,6},{6,0},{1,3},{3,5},{5,7},{7,1},{8,10},{10,12},{12... | collective-permute-start | bytes 417800 | tf_op jit(solution)/shard_map/ppermute | solution.py:283
  138.5 4.5 %collective-permute-start.3 = (bf16[2,272,128]{2,1,0:T(8,128)(2,1)S(1)}, bf16[2,272,128]{2,1,0:T(8,128)(2,1)S(1)}, u32[]{:S(2)}, u32[]{:S(2)}) collective-permute-start(bf16[2,272,128]{2,1,0:T(8,128)(2,1)S(1)} %get-tuple-element.31), channel_id=1, source_target_pairs={{0,4},{2,6},{4,0},{6,2},{1,5},{3,7},{5,1},{7,3},{8,12},{10,14},{12... | collective-permute-start | bytes 417800 | tf_op jit(solution)/shard_map/ppermute | solution.py:283
  143.0 2.7 %collective-permute-start.4 = (bf16[2,272,128]{2,1,0:T(8,128)(2,1)S(1)}, bf16[2,272,128]{2,1,0:T(8,128)(2,1)S(1)}, u32[]{:S(2)}, u32[]{:S(2)}) collective-permute-start(bf16[2,272,128]{2,1,0:T(8,128)(2,1)S(1)} %get-tuple-element.32), channel_id=1, source_target_pairs={{0,6},{2,0},{4,2},{6,4},{1,7},{3,1},{5,3},{7,5},{8,14},{10,8},{12,... | collective-permute-start | bytes 417800 | tf_op jit(solution)/shard_map/ppermute | solution.py:283
  145.7 0.0 collective-permute-done.5
  145.7 0.3 bitcast_reduce_fusion
  146.0 0.4 fusion.perturb_ref
  146.5 3.6 %collective-permute-done.2.b_ref = bf16[2,272,128]{2,1,0:T(8,128)(2,1)S(1)} collective-permute-done((bf16[2,272,128]{2,1,0:T(8,128)(2,1)S(1)}, bf16[2,272,128]{2,1,0:T(8,128)(2,1)S(1)}, u32[]{:S(2)}, u32[]{:S(2)}) %collective-permute-start.2) | collective-permute-done | bytes 139296 | tf_op jit(solution)/shard_map/ppermute | solution.py:283
  150.1 4.4 %collective-permute-done.3.c_ref = bf16[2,272,128]{2,1,0:T(8,128)(2,1)S(1)} collective-permute-done((bf16[2,272,128]{2,1,0:T(8,128)(2,1)S(1)}, bf16[2,272,128]{2,1,0:T(8,128)(2,1)S(1)}, u32[]{:S(2)}, u32[]{:S(2)}) %collective-permute-start.3) | collective-permute-done | bytes 139296 | tf_op jit(solution)/shard_map/ppermute | solution.py:283
  154.5 1.6 collective-permute-done.4.d_ref
  156.2 5.8 %weights.1 = (bf16[2,64,256]{2,1,0:T(8,128)(2,1)S(1)}, bf16[2,64,256]{2,1,0:T(8,128)(2,1)S(1)}, bf16[2,64,256]{2,1,0:T(8,128)(2,1)S(1)}, bf16[2,64,256]{2,1,0:T(8,128)(2,1)S(1)}) custom-call(bf16[2,272,128]{2,1,0:T(8,128)(2,1)S(1)} %get-tuple-element.37.a_ref, bf16[2,272,128]{2,1,0:T(8,128)(2,1)S(1)} %collective-permute-done.2.b_ref, ...), custom_call_target="tpu_custom_call" | custom-call | tf_op jit(solution)/shard_map/weights/pallas_call | solution.py:248
  162.0 0.7 collective-permute-start.6
  162.7 3.0 %collective-permute-start.7 = (bf16[2,64,256]{2,1,0:T(8,128)(2,1)S(1)}, bf16[2,64,256]{2,1,0:T(8,128)(2,1)S(1)}, u32[]{:S(2)}, u32[]{:S(2)}) collective-permute-start(bf16[2,64,256]{2,1,0:T(8,128)(2,1)S(1)} %get-tuple-element.42), channel_id=1, source_target_pairs={{0,64},{2,128},{4,192},{6,0},{64,66},{66,130},{68,194},{70,2},{128... | collective-permute-start | bytes 196616 | tf_op jit(solution)/shard_map/ppermute | solution.py:313
  165.7 6.1 %collective-permute-start.8 = (bf16[2,64,256]{2,1,0:T(8,128)(2,1)S(1)}, bf16[2,64,256]{2,1,0:T(8,128)(2,1)S(1)}, u32[]{:S(2)}, u32[]{:S(2)}) collective-permute-start(bf16[2,64,256]{2,1,0:T(8,128)(2,1)S(1)} %get-tuple-element.43), channel_id=1, source_target_pairs={{0,128},{2,192},{4,0},{6,64},{64,130},{66,194},{68,2},{70,66},{128... | collective-permute-start | bytes 196616 | tf_op jit(solution)/shard_map/ppermute | solution.py:313
  171.8 1.3 collective-permute-start.9
  173.1 0.0 collective-permute-done.6.refs_0_
  173.1 0.0 collective-permute-done.7.refs_1_
  173.1 8.1 %collective-permute-done.8.refs_2_ = bf16[2,64,256]{2,1,0:T(8,128)(2,1)S(1)} collective-permute-done((bf16[2,64,256]{2,1,0:T(8,128)(2,1)S(1)}, bf16[2,64,256]{2,1,0:T(8,128)(2,1)S(1)}, u32[]{:S(2)}, u32[]{:S(2)}) %collective-permute-start.8) | collective-permute-done | bytes 65568 | tf_op jit(solution)/shard_map/ppermute | solution.py:313
  181.2 0.0 collective-permute-done.9.refs_3_
  181.2 0.5 analysed.1
  181.7 1.1 copy.11
  (2 shorter events, 0.0 us)
Async XLA Ops:
  1.2 15.3 %collective-permute-start.1 = (bf16[64,8,512]{2,0,1:T(8,128)(2,1)S(1)}, bf16[64,8,512]{2,0,1:T(8,128)(2,1)S(1)}, u32[]{:S(2)}, u32[]{:S(2)}) collective-permute-start(bf16[64,8,512]{2,0,1:T(8,128)(2,1)S(1)} %copy.8), channel_id=1, source_target_pairs={{0,128},{64,192},{128,0},{192,64},{1,129},{65,193},{129,1},{193,65... | collective-permute-start | bytes 1572872 | tf_op jit(solution)/shard_map/ppermute | solution.py:287
  3.6 12.9 %collective-permute-start = (bf16[64,8,512]{2,0,1:T(8,128)(2,1)S(1)}, bf16[64,8,512]{2,0,1:T(8,128)(2,1)S(1)}, u32[]{:S(2)}, u32[]{:S(2)}) collective-permute-start(bf16[64,8,512]{2,0,1:T(8,128)(2,1)S(1)} %copy.8), channel_id=1, source_target_pairs={{0,64},{64,0},{128,192},{192,128},{1,65},{65,1},{129,193},{193,129... | collective-permute-start | bytes 1572872 | tf_op jit(solution)/shard_map/ppermute | solution.py:287
  127.9 17.8 %collective-permute-start.5 = (bf16[64,8,512]{2,0,1:T(8,128)(2,1)S(1)}, bf16[64,8,512]{2,0,1:T(8,128)(2,1)S(1)}, u32[]{:S(2)}, u32[]{:S(2)}) collective-permute-start(bf16[64,8,512]{2,0,1:T(8,128)(2,1)S(1)} %collective-permute-done.1), channel_id=1, source_target_pairs={{0,64},{64,0},{128,192},{192,128},{1,65},{65,1},{129,193},{193,129... | collective-permute-start | bytes 1572872 | tf_op jit(solution)/shard_map/ppermute | solution.py:287
  135.2 14.9 %collective-permute-start.2 = (bf16[2,272,128]{2,1,0:T(8,128)(2,1)S(1)}, bf16[2,272,128]{2,1,0:T(8,128)(2,1)S(1)}, u32[]{:S(2)}, u32[]{:S(2)}) collective-permute-start(bf16[2,272,128]{2,1,0:T(8,128)(2,1)S(1)} %get-tuple-element.30), channel_id=1, source_target_pairs={{0,2},{2,4},{4,6},{6,0},{1,3},{3,5},{5,7},{7,1},{8,10},{10,12},{12... | collective-permute-start | bytes 417800 | tf_op jit(solution)/shard_map/ppermute | solution.py:283
  138.5 16.0 %collective-permute-start.3 = (bf16[2,272,128]{2,1,0:T(8,128)(2,1)S(1)}, bf16[2,272,128]{2,1,0:T(8,128)(2,1)S(1)}, u32[]{:S(2)}, u32[]{:S(2)}) collective-permute-start(bf16[2,272,128]{2,1,0:T(8,128)(2,1)S(1)} %get-tuple-element.31), channel_id=1, source_target_pairs={{0,4},{2,6},{4,0},{6,2},{1,5},{3,7},{5,1},{7,3},{8,12},{10,14},{12... | collective-permute-start | bytes 417800 | tf_op jit(solution)/shard_map/ppermute | solution.py:283
  143.0 13.2 %collective-permute-start.4 = (bf16[2,272,128]{2,1,0:T(8,128)(2,1)S(1)}, bf16[2,272,128]{2,1,0:T(8,128)(2,1)S(1)}, u32[]{:S(2)}, u32[]{:S(2)}) collective-permute-start(bf16[2,272,128]{2,1,0:T(8,128)(2,1)S(1)} %get-tuple-element.32), channel_id=1, source_target_pairs={{0,6},{2,0},{4,2},{6,4},{1,7},{3,1},{5,3},{7,5},{8,14},{10,8},{12,... | collective-permute-start | bytes 417800 | tf_op jit(solution)/shard_map/ppermute | solution.py:283
  162.0 11.1 %collective-permute-start.6 = (bf16[2,64,256]{2,1,0:T(8,128)(2,1)S(1)}, bf16[2,64,256]{2,1,0:T(8,128)(2,1)S(1)}, u32[]{:S(2)}, u32[]{:S(2)}) collective-permute-start(bf16[2,64,256]{2,1,0:T(8,128)(2,1)S(1)} %get-tuple-element.41), channel_id=1, source_target_pairs={{0,0},{2,64},{4,128},{6,192},{64,2},{66,66},{68,130},{70,194},{128... | collective-permute-start | bytes 196616 | tf_op jit(solution)/shard_map/ppermute | solution.py:313
  162.7 10.4 %collective-permute-start.7 = (bf16[2,64,256]{2,1,0:T(8,128)(2,1)S(1)}, bf16[2,64,256]{2,1,0:T(8,128)(2,1)S(1)}, u32[]{:S(2)}, u32[]{:S(2)}) collective-permute-start(bf16[2,64,256]{2,1,0:T(8,128)(2,1)S(1)} %get-tuple-element.42), channel_id=1, source_target_pairs={{0,64},{2,128},{4,192},{6,0},{64,66},{66,130},{68,194},{70,2},{128... | collective-permute-start | bytes 196616 | tf_op jit(solution)/shard_map/ppermute | solution.py:313
  165.7 15.5 %collective-permute-start.8 = (bf16[2,64,256]{2,1,0:T(8,128)(2,1)S(1)}, bf16[2,64,256]{2,1,0:T(8,128)(2,1)S(1)}, u32[]{:S(2)}, u32[]{:S(2)}) collective-permute-start(bf16[2,64,256]{2,1,0:T(8,128)(2,1)S(1)} %get-tuple-element.43), channel_id=1, source_target_pairs={{0,128},{2,192},{4,0},{6,64},{64,130},{66,194},{68,2},{70,66},{128... | collective-permute-start | bytes 196616 | tf_op jit(solution)/shard_map/ppermute | solution.py:313
  171.8 9.4 %collective-permute-start.9 = (bf16[2,64,256]{2,1,0:T(8,128)(2,1)S(1)}, bf16[2,64,256]{2,1,0:T(8,128)(2,1)S(1)}, u32[]{:S(2)}, u32[]{:S(2)}) collective-permute-start(bf16[2,64,256]{2,1,0:T(8,128)(2,1)S(1)} %get-tuple-element.44), channel_id=1, source_target_pairs={{0,192},{2,0},{4,64},{6,128},{64,194},{66,2},{68,66},{70,130},{128... | collective-permute-start | bytes 196616 | tf_op jit(solution)/shard_map/ppermute | solution.py:313

commit v2 on v1

--- a/solution.py
+++ b/solution.py
@@ -9,12 +9,13 @@
 from jax.sharding import Mesh
 from jax.sharding import PartitionSpec as P
 
+
 SAMPLE_NUMBER = 256
 OB = 128
 CAP = 2
 PATCH_REG = 8
 ITERS = 5
-META = 16
+META = 8
 ROWS = CAP * OB + META
 HALF = SAMPLE_NUMBER // 2
 MEMBERS = SAMPLE_NUMBER // 4
@@ -199,7 +200,7 @@
 
 
 def newton_kernel(a_ref, b_ref, c_ref, d_ref, *refs):
-    zq = lax.axis_index("zq")
+    mem = lax.axis_index("mem")
     outs, (gram_ref, weight_ref) = refs[:4], refs[4:]
     row = lax.broadcasted_iota(jnp.int32, (HALF, HALF), 0)
     col = lax.broadcasted_iota(jnp.int32, (HALF, HALF), 1)
@@ -223,7 +224,7 @@
         frob = jnp.sqrt(squares)
         root = gram / frob
         inverse = step = 1.5 * identity - 0.5 * root
-        for sweep in range(1, ITERS):
+        for _ in range(1, ITERS):
             step_parts = split(step)
             root = product(split(root), step_parts)
             inverse_parts = split(inverse)
@@ -234,7 +235,7 @@
         mean_weight = jnp.sum(inv_root * once, axis=0, keepdims=True)
         weight_ref[...] = math.sqrt(SAMPLE_NUMBER - 1.0) * inv_root + mean_weight
         for e in range(4):
-            goal = (zq + e) % 4
+            goal = mem ^ e
             part = weight_ref[pl.ds(pl.multiple_of(goal * MEMBERS, MEMBERS), MEMBERS), :]
             low, high = part[:, :HALF], part[:, HALF:]
             low, high = jnp.where(goal >= 2, high, low), jnp.where(goal >= 2, low, high)
@@ -262,7 +263,7 @@
     mem = lax.axis_index("mem")
     for e in range(4):
         for i in range(2):
-            p = (mem - e + 4) % 4 * 2 + i
+            p = (mem ^ e) * 2 + i
             update = jnp.dot(routed[e][i], perturb_ref[p], preferred_element_type=jnp.float32)
             out_ref[p] = (mean_ref[p] + update).astype(jnp.bfloat16)
 
@@ -278,13 +279,13 @@
     )(perturb, state_mean, *routed)
 
 
-def shift(x, axis, by):
-    n = lax.axis_size(axis)
-    return lax.ppermute(x, axis, [(j, (j + by) % n) for j in range(n)])
-
-
 def swap(x, bit):
     return lax.ppermute(x, "mem", [(j, j ^ bit) for j in range(4)])
+
+
+def to_owner(x, e):
+    pairs = [(m * 4 + z, (z + e) % 4 * 4 + m) for m in range(4) for z in range(4)]
+    return lax.ppermute(x, ("mem", "zq"), pairs)
 
 
 def per_device(prior, anomalies, spread, departure, tally, zone, tile):
@@ -294,29 +295,20 @@
         *(in_hbm(x) for x in (anomalies, spread, departure, tally, tile, zone[:, 0])),
         (ways["zq"], ways["ylo"] * ways["x"], ways["zp"]),
     )
+    arrived = lax.all_to_all(messages, GROUP, split_axis=0, concat_axis=0, tiled=True)
+
+    pieces = partial_grams(arrived)
+    pieces, prior = lax.optimization_barrier((pieces, prior))
+    pieces = [to_owner(pieces[e], e) for e in range(4)]
+
     near, far = swap(prior, 1), swap(prior, 2)
-    messages, near, far = lax.optimization_barrier((messages, near, far))
-    arrived = lax.all_to_all(messages, GROUP, split_axis=0, concat_axis=0, tiled=True)
-    arrived, near, far = lax.optimization_barrier((arrived, near, far))
     farther = swap(far, 1)
-
-    pieces = partial_grams(arrived)
-    pieces = [pieces[0]] + [shift(pieces[d], "zq", d) for d in range(1, 4)]
-
     field = jnp.concatenate([prior, near, far, farther], axis=0).transpose(1, 0, 2)
     state_mean = jnp.sum(field, axis=1, keepdims=True, dtype=jnp.float32) / SAMPLE_NUMBER
     perturb = (field - state_mean).astype(jnp.bfloat16)
-    pieces, state_mean, perturb = lax.optimization_barrier((pieces, state_mean, perturb))
+
     weights = flipped_weights(pieces)
-
-    routed = [
-        lax.ppermute(
-            weights[e],
-            ("mem", "zq"),
-            [(m * 4 + z, (z + e) % 4 * 4 + m) for m in range(4) for z in range(4)],
-        )
-        for e in range(4)
-    ]
+    routed = [weights[0]] + [swap(weights[e], e) for e in range(1, 4)]
     return analysed(perturb, state_mean, routed).transpose(1, 0, 2)
 
 

time: 185 us -> 190 us (1.027)
  starting transfers between devices: 24 us -> 33.5 us
  waiting for transfers between devices: 26.2 us -> 23.3 us
  blocking collectives: 111 us -> 109 us
    ppermute x7 -> x4, waiting for transfers between devices: 17.8 us -> 4.05 us  [to_owner(): return lax.ppermute(x, ('mem', 'zq'), pairs)]
    ppermute x3 -> x6, waiting for transfers between devices: 8.39 us -> 19.3 us  [swap(): return lax.ppermute(x, 'mem', [(j, j ^ bit) for j in range(4)])]
    ppermute x7 -> x4, starting transfers between devices: 21.6 us -> 28.6 us  [to_owner(): return lax.ppermute(x, ('mem', 'zq'), pairs)]
    ppermute x3 -> x6, starting transfers between devices: 2.4 us -> 4.85 us  [swap(): return lax.ppermute(x, 'mem', [(j, j ^ bit) for j in range(4)])]
    all_to_all x1, blocking collectives: 111 us -> 109 us  [per_device(): lax.all_to_all(messages, GROUP, split_axis=0, concat_axis=0, tiled=True)]
  transfers between devices with their start and end apart: 10 -> 10, of which waited for: 5 -> 5; matrix products, arithmetic and copies ran while one was open for 0% -> 0% of each run, Pallas kernels for 6% -> 3%
where the time goes in v2:
time: 190 us; the launch traced here: 186 us
  blocking collectives  109 us (57%)
  starting transfers between devices  33.5 us (18%)
  waiting for transfers between devices  23.3 us (12%)
  Pallas kernels  18.2 us (10%)
    all_to_all x1, blocking collectives, per_device(): lax.all_to_all(messages, GROUP, split_axis=0, concat_axis=0, tiled=True)  109 us
    ppermute x4, starting transfers between devices, to_owner(): return lax.ppermute(x, ('mem', 'zq'), pairs)  28.6 us
    ppermute x6, waiting for transfers between devices, swap(): return lax.ppermute(x, 'mem', [(j, j ^ bit) for j in range(4)])  19.3 us
    pallas_call x1, Pallas kernels, partial_grams(): pl.pallas_call(gram_kernel, out_shape=[piece] * 4, grid_spec=pl.GridSpec(...  7.44 us
    pallas_call x1, Pallas kernels, flipped_weights(): pl.pallas_call(newton_kernel, out_shape=[piece] * 4, scratch_shapes=[pltp...  5.84 us
    ppermute x6, starting transfers between devices, swap(): return lax.ppermute(x, 'mem', [(j, j ^ bit) for j in range(4)])  4.85 us
    pallas_call x1, Pallas kernels, build_messages(): pl.pallas_call(functools.partial(prep_kernel, ways), out_shape=jax.ShapeD...  4.45 us
    ppermute x4, waiting for transfers between devices, to_owner(): return lax.ppermute(x, ('mem', 'zq'), pairs)  4.05 us
  transfers between devices with their start and end apart: 10, of which 5 were waited for; matrix products, arithmetic and copies ran while one was open for 0% of the time, Pallas kernels for 3%

profile of v2, /device:TPU:40, one launch (start us, length us, event | category | flops | bytes accessed | tf_op | source)
XLA Modules:
  0.0 186.3 jit_solution(11696863024508394574)
XLA Ops:
  0.0 4.4 %build_messages.1 = bf16[64,264,256]{2,1,0:T(8,128)(2,1)S(1)} custom-call(s32[64]{0:T(128)} %bitcast.8, s32[64]{0:T(128)} %tally_smem.1, s32[64]{0:T(128)} %tile_smem.1, bf16[64,128,256]{2,1,0:T(8,128)(2,1)} %anom_ref.1, f32[64,128]{1,0:T(8,128)} %spread_ref.1, f32[64,128]{1,0:T(8,128)} %depart_ref.1), custom_call_target="tpu_custom_call" | custom-call | bytes 8388608 | tf_op jit(solution)/shard_map/build_messages/pallas_call | solution.py:83
  4.5 109.2 %all_to_all.5.tag_ref.rows_ref = bf16[64,264,256]{2,1,0:T(8,128)(2,1)S(1)} all-to-all(bf16[64,264,256]{2,1,0:T(8,128)(2,1)S(1)} %build_messages.1), channel_id=1, replica_groups=mesh['mem'=4,'ylo'=2,'x'=4,'zq'=4,'zp'=2] {'mem','ylo','x','zp'}, dimensions={0} | all-to-all | bytes 17301504 | tf_op jit(solution)/shard_map/all_to_all | solution.py:298
  113.6 0.0 copy-start
  113.6 7.4 %partial_grams.1 = (bf16[2,272,128]{2,1,0:T(8,128)(2,1)S(1)}, bf16[2,272,128]{2,1,0:T(8,128)(2,1)S(1)}, bf16[2,272,128]{2,1,0:T(8,128)(2,1)S(1)}, bf16[2,272,128]{2,1,0:T(8,128)(2,1)S(1)}) custom-call(bf16[64,264,256]{2,1,0:T(8,128)(2,1)S(1)} %all_to_all.5.tag_ref.rows_ref, bf16[64,264,256]{2,1,0:T(8,128)(2,1)S(1)} %all_to_all.5.tag_ref.rows_ref), custom_call_target="tpu_custom_call" | custom-call | flops 2147483648 | bytes 8388608 | tf_op jit(solution)/shard_map/partial_grams/pallas_call | solution.py:168
  121.1 0.0 copy-done
  121.1 0.2 copy.10
  121.2 1.0 collective-permute-start.1
  122.2 0.0 collective-permute-start
  122.2 14.2 %collective-permute-done.1 = bf16[64,8,512]{2,0,1:T(8,128)(2,1)S(1)} collective-permute-done((bf16[64,8,512]{2,0,1:T(8,128)(2,1)S(1)}, bf16[64,8,512]{2,0,1:T(8,128)(2,1)S(1)}, u32[]{:S(2)}, u32[]{:S(2)}) %collective-permute-start.1) | collective-permute-done | bytes 524320 | tf_op jit(solution)/shard_map/ppermute | solution.py:283
  136.4 0.0 collective-permute-start.2
  136.4 0.7 collective-permute-start.3
  137.1 4.7 %collective-permute-start.4 = (bf16[2,272,128]{2,1,0:T(8,128)(2,1)S(1)}, bf16[2,272,128]{2,1,0:T(8,128)(2,1)S(1)}, u32[]{:S(2)}, u32[]{:S(2)}) collective-permute-start(bf16[2,272,128]{2,1,0:T(8,128)(2,1)S(1)} %get-tuple-element.24), channel_id=1, source_target_pairs={{0,64},{2,128},{4,192},{6,0},{64,66},{66,130},{68,194},{70,2},{128... | collective-permute-start | bytes 417800 | tf_op jit(solution)/shard_map/ppermute | solution.py:288
  141.8 6.6 %collective-permute-start.5 = (bf16[2,272,128]{2,1,0:T(8,128)(2,1)S(1)}, bf16[2,272,128]{2,1,0:T(8,128)(2,1)S(1)}, u32[]{:S(2)}, u32[]{:S(2)}) collective-permute-start(bf16[2,272,128]{2,1,0:T(8,128)(2,1)S(1)} %get-tuple-element.25), channel_id=1, source_target_pairs={{0,128},{2,192},{4,0},{6,64},{64,130},{66,194},{68,2},{70,66},{128... | collective-permute-start | bytes 417800 | tf_op jit(solution)/shard_map/ppermute | solution.py:288
  148.3 0.0 collective-permute-done.3.a_ref
  148.4 16.7 %collective-permute-start.6 = (bf16[2,272,128]{2,1,0:T(8,128)(2,1)S(1)}, bf16[2,272,128]{2,1,0:T(8,128)(2,1)S(1)}, u32[]{:S(2)}, u32[]{:S(2)}) collective-permute-start(bf16[2,272,128]{2,1,0:T(8,128)(2,1)S(1)} %get-tuple-element.26), channel_id=1, source_target_pairs={{0,192},{2,0},{4,64},{6,128},{64,194},{66,2},{68,66},{70,130},{128... | collective-permute-start | bytes 417800 | tf_op jit(solution)/shard_map/ppermute | solution.py:288
  165.0 0.6 collective-permute-done.4.b_ref
  165.6 0.0 collective-permute-done.5.c_ref
  165.6 3.5 %collective-permute-done.6.d_ref = bf16[2,272,128]{2,1,0:T(8,128)(2,1)S(1)} collective-permute-done((bf16[2,272,128]{2,1,0:T(8,128)(2,1)S(1)}, bf16[2,272,128]{2,1,0:T(8,128)(2,1)S(1)}, u32[]{:S(2)}, u32[]{:S(2)}) %collective-permute-start.6) | collective-permute-done | bytes 139296 | tf_op jit(solution)/shard_map/ppermute | solution.py:288
  169.1 5.8 %weights.1 = (bf16[2,64,256]{2,1,0:T(8,128)(2,1)S(1)}, bf16[2,64,256]{2,1,0:T(8,128)(2,1)S(1)}, bf16[2,64,256]{2,1,0:T(8,128)(2,1)S(1)}, bf16[2,64,256]{2,1,0:T(8,128)(2,1)S(1)}) custom-call(bf16[2,272,128]{2,1,0:T(8,128)(2,1)S(1)} %collective-permute-done.3.a_ref, bf16[2,272,128]{2,1,0:T(8,128)(2,1)S(1)} %collective-permute-done.4.b_ref, ...), custom_call_target="tpu_custom_call" | custom-call | tf_op jit(solution)/shard_map/weights/pallas_call | solution.py:249
  174.9 0.1 collective-permute-start.7
  175.0 3.8 %collective-permute-start.8 = (bf16[2,64,256]{2,1,0:T(8,128)(2,1)S(1)}, bf16[2,64,256]{2,1,0:T(8,128)(2,1)S(1)}, u32[]{:S(2)}, u32[]{:S(2)}) collective-permute-start(bf16[2,64,256]{2,1,0:T(8,128)(2,1)S(1)} %get-tuple-element.29), channel_id=1, source_target_pairs={{0,128},{64,192},{128,0},{192,64},{1,129},{65,193},{129,1},{193,65... | collective-permute-start | bytes 196616 | tf_op jit(solution)/shard_map/ppermute | solution.py:283
  178.8 0.0 collective-permute-start.9
  178.8 0.0 collective-permute-done
  178.8 0.0 collective-permute-done.2
  178.8 0.3 bitcast_reduce_fusion
  179.2 0.4 fusion.perturb_ref
  179.6 0.0 collective-permute-done.7.refs_1_
  179.6 1.5 collective-permute-done.8.refs_2_
  181.2 3.5 %collective-permute-done.9.refs_3_ = bf16[2,64,256]{2,1,0:T(8,128)(2,1)S(1)} collective-permute-done((bf16[2,64,256]{2,1,0:T(8,128)(2,1)S(1)}, bf16[2,64,256]{2,1,0:T(8,128)(2,1)S(1)}, u32[]{:S(2)}, u32[]{:S(2)}) %collective-permute-start.9) | collective-permute-done | bytes 65568 | tf_op jit(solution)/shard_map/ppermute | solution.py:283
  184.7 0.5 analysed.1
  185.2 1.1 copy.11
  (2 shorter events, 0.0 us)
Async XLA Ops:
  113.6 7.4 %copy-start = (bf16[64,8,512]{2,1,0:T(8,128)(2,1)S(1)}, bf16[64,8,512]{2,1,0:T(8,128)(2,1)}, u32[]{:S(2)}) copy-start(bf16[64,8,512]{2,1,0:T(8,128)(2,1)} %param.7) | copy-start | bytes 1572868
  121.2 15.2 %collective-permute-start.1 = (bf16[64,8,512]{2,0,1:T(8,128)(2,1)S(1)}, bf16[64,8,512]{2,0,1:T(8,128)(2,1)S(1)}, u32[]{:S(2)}, u32[]{:S(2)}) collective-permute-start(bf16[64,8,512]{2,0,1:T(8,128)(2,1)S(1)} %copy.10), channel_id=1, source_target_pairs={{0,128},{64,192},{128,0},{192,64},{1,129},{65,193},{129,1},{193,65... | collective-permute-start | bytes 1572872 | tf_op jit(solution)/shard_map/ppermute | solution.py:283
  122.2 56.6 %collective-permute-start = (bf16[64,8,512]{2,0,1:T(8,128)(2,1)S(1)}, bf16[64,8,512]{2,0,1:T(8,128)(2,1)S(1)}, u32[]{:S(2)}, u32[]{:S(2)}) collective-permute-start(bf16[64,8,512]{2,0,1:T(8,128)(2,1)S(1)} %copy.10), channel_id=1, source_target_pairs={{0,64},{64,0},{128,192},{192,128},{1,65},{65,1},{129,193},{193,129... | collective-permute-start | bytes 1572872 | tf_op jit(solution)/shard_map/ppermute | solution.py:283
  136.4 42.4 %collective-permute-start.2 = (bf16[64,8,512]{2,0,1:T(8,128)(2,1)S(1)}, bf16[64,8,512]{2,0,1:T(8,128)(2,1)S(1)}, u32[]{:S(2)}, u32[]{:S(2)}) collective-permute-start(bf16[64,8,512]{2,0,1:T(8,128)(2,1)S(1)} %collective-permute-done.1), channel_id=1, source_target_pairs={{0,64},{64,0},{128,192},{192,128},{1,65},{65,1},{129,193},{193,129... | collective-permute-start | bytes 1572872 | tf_op jit(solution)/shard_map/ppermute | solution.py:283
  136.4 11.9 %collective-permute-start.3 = (bf16[2,272,128]{2,1,0:T(8,128)(2,1)S(1)}, bf16[2,272,128]{2,1,0:T(8,128)(2,1)S(1)}, u32[]{:S(2)}, u32[]{:S(2)}) collective-permute-start(bf16[2,272,128]{2,1,0:T(8,128)(2,1)S(1)} %get-tuple-element.23), channel_id=1, source_target_pairs={{0,0},{2,64},{4,128},{6,192},{64,2},{66,66},{68,130},{70,194},{128... | collective-permute-start | bytes 417800 | tf_op jit(solution)/shard_map/ppermute | solution.py:288
  137.1 28.5 %collective-permute-start.4 = (bf16[2,272,128]{2,1,0:T(8,128)(2,1)S(1)}, bf16[2,272,128]{2,1,0:T(8,128)(2,1)S(1)}, u32[]{:S(2)}, u32[]{:S(2)}) collective-permute-start(bf16[2,272,128]{2,1,0:T(8,128)(2,1)S(1)} %get-tuple-element.24), channel_id=1, source_target_pairs={{0,64},{2,128},{4,192},{6,0},{64,66},{66,130},{68,194},{70,2},{128... | collective-permute-start | bytes 417800 | tf_op jit(solution)/shard_map/ppermute | solution.py:288
  141.8 23.8 %collective-permute-start.5 = (bf16[2,272,128]{2,1,0:T(8,128)(2,1)S(1)}, bf16[2,272,128]{2,1,0:T(8,128)(2,1)S(1)}, u32[]{:S(2)}, u32[]{:S(2)}) collective-permute-start(bf16[2,272,128]{2,1,0:T(8,128)(2,1)S(1)} %get-tuple-element.25), channel_id=1, source_target_pairs={{0,128},{2,192},{4,0},{6,64},{64,130},{66,194},{68,2},{70,66},{128... | collective-permute-start | bytes 417800 | tf_op jit(solution)/shard_map/ppermute | solution.py:288
  148.4 20.7 %collective-permute-start.6 = (bf16[2,272,128]{2,1,0:T(8,128)(2,1)S(1)}, bf16[2,272,128]{2,1,0:T(8,128)(2,1)S(1)}, u32[]{:S(2)}, u32[]{:S(2)}) collective-permute-start(bf16[2,272,128]{2,1,0:T(8,128)(2,1)S(1)} %get-tuple-element.26), channel_id=1, source_target_pairs={{0,192},{2,0},{4,64},{6,128},{64,194},{66,2},{68,66},{70,130},{128... | collective-permute-start | bytes 417800 | tf_op jit(solution)/shard_map/ppermute | solution.py:288
  174.9 4.7 %collective-permute-start.7 = (bf16[2,64,256]{2,1,0:T(8,128)(2,1)S(1)}, bf16[2,64,256]{2,1,0:T(8,128)(2,1)S(1)}, u32[]{:S(2)}, u32[]{:S(2)}) collective-permute-start(bf16[2,64,256]{2,1,0:T(8,128)(2,1)S(1)} %get-tuple-element.28), channel_id=1, source_target_pairs={{0,64},{64,0},{128,192},{192,128},{1,65},{65,1},{129,193},{193,129... | collective-permute-start | bytes 196616 | tf_op jit(solution)/shard_map/ppermute | solution.py:283
  175.0 6.2 %collective-permute-start.8 = (bf16[2,64,256]{2,1,0:T(8,128)(2,1)S(1)}, bf16[2,64,256]{2,1,0:T(8,128)(2,1)S(1)}, u32[]{:S(2)}, u32[]{:S(2)}) collective-permute-start(bf16[2,64,256]{2,1,0:T(8,128)(2,1)S(1)} %get-tuple-element.29), channel_id=1, source_target_pairs={{0,128},{64,192},{128,0},{192,64},{1,129},{65,193},{129,1},{193,65... | collective-permute-start | bytes 196616 | tf_op jit(solution)/shard_map/ppermute | solution.py:283
  178.8 5.9 %collective-permute-start.9 = (bf16[2,64,256]{2,1,0:T(8,128)(2,1)S(1)}, bf16[2,64,256]{2,1,0:T(8,128)(2,1)S(1)}, u32[]{:S(2)}, u32[]{:S(2)}) collective-permute-start(bf16[2,64,256]{2,1,0:T(8,128)(2,1)S(1)} %get-tuple-element.30), channel_id=1, source_target_pairs={{0,192},{64,128},{128,64},{192,0},{1,193},{65,129},{129,65},{193,1... | collective-permute-start | bytes 196616 | tf_op jit(solution)/shard_map/ppermute | solution.py:283

commit v3 on v2

--- a/solution.py
+++ b/solution.py
@@ -297,18 +297,18 @@
     )
     arrived = lax.all_to_all(messages, GROUP, split_axis=0, concat_axis=0, tiled=True)
 
+    arrived, prior = lax.optimization_barrier((arrived, prior))
+    near, far = swap(prior, 1), swap(prior, 2)
+
     pieces = partial_grams(arrived)
-    pieces, prior = lax.optimization_barrier((pieces, prior))
-    pieces = [to_owner(pieces[e], e) for e in range(4)]
-
-    near, far = swap(prior, 1), swap(prior, 2)
+    weights = flipped_weights([to_owner(pieces[e], e) for e in range(4)])
+
+    weights, far = lax.optimization_barrier((weights, far))
+    routed = [weights[0]] + [swap(weights[e], e) for e in range(1, 4)]
     farther = swap(far, 1)
     field = jnp.concatenate([prior, near, far, farther], axis=0).transpose(1, 0, 2)
     state_mean = jnp.sum(field, axis=1, keepdims=True, dtype=jnp.float32) / SAMPLE_NUMBER
     perturb = (field - state_mean).astype(jnp.bfloat16)
-
-    weights = flipped_weights(pieces)
-    routed = [weights[0]] + [swap(weights[e], e) for e in range(1, 4)]
     return analysed(perturb, state_mean, routed).transpose(1, 0, 2)
 
 

time: 190 us -> 173 us (0.911); the launches traced: 186 us -> 171 us
  starting transfers between devices: 33.5 us -> 21.1 us
  waiting for transfers between devices: 23.3 us -> 20.6 us
    ppermute x4, starting transfers between devices: 28.6 us -> 13.7 us  [to_owner(): return lax.ppermute(x, ('mem', 'zq'), pairs)]
    ppermute x6, waiting for transfers between devices: 19.3 us -> 5.09 us  [swap(): return lax.ppermute(x, 'mem', [(j, j ^ bit) for j in range(4)])]
    ppermute x4, waiting for transfers between devices: 4.05 us -> 15.5 us  [to_owner(): return lax.ppermute(x, ('mem', 'zq'), pairs)]
    ppermute x6, starting transfers between devices: 4.85 us -> 7.44 us  [swap(): return lax.ppermute(x, 'mem', [(j, j ^ bit) for j in range(4)])]
  transfers between devices with their start and end apart: 10 -> 10, of which waited for: 5 -> 3; matrix products, arithmetic and copies ran while one was open for 0% -> 0% of each run, Pallas kernels for 3% -> 8%
where the time goes in v3:
time: 173 us; the launch traced here: 171 us
  blocking collectives  109 us (63%)
  starting transfers between devices  21.1 us (12%)
  waiting for transfers between devices  20.6 us (12%)
  Pallas kernels  18.2 us (11%)
    all_to_all x1, blocking collectives, per_device(): lax.all_to_all(messages, GROUP, split_axis=0, concat_axis=0, tiled=True)  109 us
    ppermute x4, waiting for transfers between devices, to_owner(): return lax.ppermute(x, ('mem', 'zq'), pairs)  15.5 us
    ppermute x4, starting transfers between devices, to_owner(): return lax.ppermute(x, ('mem', 'zq'), pairs)  13.7 us
    ppermute x6, starting transfers between devices, swap(): return lax.ppermute(x, 'mem', [(j, j ^ bit) for j in range(4)])  7.44 us
    pallas_call x1, Pallas kernels, partial_grams(): pl.pallas_call(gram_kernel, out_shape=[piece] * 4, grid_spec=pl.GridSpec(...  7.42 us
    pallas_call x1, Pallas kernels, flipped_weights(): pl.pallas_call(newton_kernel, out_shape=[piece] * 4, scratch_shapes=[pltp...  5.84 us
    ppermute x6, waiting for transfers between devices, swap(): return lax.ppermute(x, 'mem', [(j, j ^ bit) for j in range(4)])  5.09 us
    pallas_call x1, Pallas kernels, build_messages(): pl.pallas_call(functools.partial(prep_kernel, ways), out_shape=jax.ShapeD...  4.45 us
  transfers between devices with their start and end apart: 10, of which 3 were waited for; matrix products, arithmetic and copies ran while one was open for 0% of the time, Pallas kernels for 8%

profile of v3, /device:TPU:40, one launch (start us, length us, event | category | flops | bytes accessed | tf_op | source)
XLA Modules:
  0.0 171.3 jit_solution(4954679075042575503)
XLA Ops:
  0.0 4.4 %build_messages.1 = bf16[64,264,256]{2,1,0:T(8,128)(2,1)S(1)} custom-call(s32[64]{0:T(128)} %bitcast.8, s32[64]{0:T(128)} %tally_smem.1, s32[64]{0:T(128)} %tile_smem.1, bf16[64,128,256]{2,1,0:T(8,128)(2,1)} %anom_ref.1, f32[64,128]{1,0:T(8,128)} %spread_ref.1, f32[64,128]{1,0:T(8,128)} %depart_ref.1), custom_call_target="tpu_custom_call" | custom-call | bytes 8388608 | tf_op jit(solution)/shard_map/build_messages/pallas_call | solution.py:83
  4.5 0.0 copy-start
  4.5 109.3 %all_to_all.5.tag_ref.rows_ref = bf16[64,264,256]{2,1,0:T(8,128)(2,1)S(1)} all-to-all(bf16[64,264,256]{2,1,0:T(8,128)(2,1)S(1)} %build_messages.1), channel_id=1, replica_groups=mesh['mem'=4,'ylo'=2,'x'=4,'zq'=4,'zp'=2] {'mem','ylo','x','zp'}, dimensions={0} | all-to-all | bytes 17301504 | tf_op jit(solution)/shard_map/all_to_all | solution.py:298
  113.8 0.0 copy-done
  113.8 0.2 copy.10
  113.9 0.9 collective-permute-start.5
  114.8 7.4 %partial_grams.1 = (bf16[2,272,128]{2,1,0:T(8,128)(2,1)S(1)}, bf16[2,272,128]{2,1,0:T(8,128)(2,1)S(1)}, bf16[2,272,128]{2,1,0:T(8,128)(2,1)S(1)}, bf16[2,272,128]{2,1,0:T(8,128)(2,1)S(1)}) custom-call(bf16[64,264,256]{2,1,0:T(8,128)(2,1)S(1)} %all_to_all.5.tag_ref.rows_ref, bf16[64,264,256]{2,1,0:T(8,128)(2,1)S(1)} %all_to_all.5.tag_ref.rows_ref), custom_call_target="tpu_custom_call" | custom-call | flops 2147483648 | bytes 8388608 | tf_op jit(solution)/shard_map/partial_grams/pallas_call | solution.py:168
  122.3 0.7 collective-permute-start.1
  122.9 4.7 %collective-permute-start.2 = (bf16[2,272,128]{2,1,0:T(8,128)(2,1)S(1)}, bf16[2,272,128]{2,1,0:T(8,128)(2,1)S(1)}, u32[]{:S(2)}, u32[]{:S(2)}) collective-permute-start(bf16[2,272,128]{2,1,0:T(8,128)(2,1)S(1)} %get-tuple-element.23), channel_id=1, source_target_pairs={{0,64},{2,128},{4,192},{6,0},{64,66},{66,130},{68,194},{70,2},{128... | collective-permute-start | bytes 417800 | tf_op jit(solution)/shard_map/ppermute | solution.py:288
  127.7 8.3 %collective-permute-start.3 = (bf16[2,272,128]{2,1,0:T(8,128)(2,1)S(1)}, bf16[2,272,128]{2,1,0:T(8,128)(2,1)S(1)}, u32[]{:S(2)}, u32[]{:S(2)}) collective-permute-start(bf16[2,272,128]{2,1,0:T(8,128)(2,1)S(1)} %get-tuple-element.24), channel_id=1, source_target_pairs={{0,128},{2,192},{4,0},{6,64},{64,130},{66,194},{68,2},{70,66},{128... | collective-permute-start | bytes 417800 | tf_op jit(solution)/shard_map/ppermute | solution.py:288
  136.0 0.0 collective-permute-start.4
  136.0 0.0 collective-permute-done.1.a_ref
  136.0 0.0 collective-permute-start
  136.0 15.5 %collective-permute-done.2.b_ref = bf16[2,272,128]{2,1,0:T(8,128)(2,1)S(1)} collective-permute-done((bf16[2,272,128]{2,1,0:T(8,128)(2,1)S(1)}, bf16[2,272,128]{2,1,0:T(8,128)(2,1)S(1)}, u32[]{:S(2)}, u32[]{:S(2)}) %collective-permute-start.2) | collective-permute-done | bytes 139296 | tf_op jit(solution)/shard_map/ppermute | solution.py:288
  151.5 0.0 collective-permute-done.3.c_ref
  151.5 0.0 collective-permute-done.4.d_ref
  151.5 5.8 %weights.1 = (bf16[2,64,256]{2,1,0:T(8,128)(2,1)S(1)}, bf16[2,64,256]{2,1,0:T(8,128)(2,1)S(1)}, bf16[2,64,256]{2,1,0:T(8,128)(2,1)S(1)}, bf16[2,64,256]{2,1,0:T(8,128)(2,1)S(1)}) custom-call(bf16[2,272,128]{2,1,0:T(8,128)(2,1)S(1)} %collective-permute-done.1.a_ref, bf16[2,272,128]{2,1,0:T(8,128)(2,1)S(1)} %collective-permute-done.2.b_ref, ...), custom_call_target="tpu_custom_call" | custom-call | tf_op jit(solution)/shard_map/weights/pallas_call | solution.py:249
  157.3 0.0 collective-permute-done.5
  157.3 1.4 collective-permute-start.6
  158.7 0.1 collective-permute-start.7
  158.8 5.0 %collective-permute-start.8 = (bf16[2,64,256]{2,1,0:T(8,128)(2,1)S(1)}, bf16[2,64,256]{2,1,0:T(8,128)(2,1)S(1)}, u32[]{:S(2)}, u32[]{:S(2)}) collective-permute-start(bf16[2,64,256]{2,1,0:T(8,128)(2,1)S(1)} %get-tuple-element.33), channel_id=1, source_target_pairs={{0,128},{64,192},{128,0},{192,64},{1,129},{65,193},{129,1},{193,65... | collective-permute-start | bytes 196616 | tf_op jit(solution)/shard_map/ppermute | solution.py:283
  163.9 0.0 collective-permute-start.9
  163.9 0.0 collective-permute-done
  163.9 0.0 collective-permute-done.6
  163.9 0.3 bitcast_reduce_fusion
  164.2 0.4 fusion.perturb_ref
  164.7 0.0 collective-permute-done.7.refs_1_
  164.7 1.5 collective-permute-done.8.refs_2_
  166.2 3.5 %collective-permute-done.9.refs_3_ = bf16[2,64,256]{2,1,0:T(8,128)(2,1)S(1)} collective-permute-done((bf16[2,64,256]{2,1,0:T(8,128)(2,1)S(1)}, bf16[2,64,256]{2,1,0:T(8,128)(2,1)S(1)}, u32[]{:S(2)}, u32[]{:S(2)}) %collective-permute-start.9) | collective-permute-done | bytes 65568 | tf_op jit(solution)/shard_map/ppermute | solution.py:283
  169.8 0.5 analysed.1
  170.2 1.1 copy.11
  (2 shorter events, 0.0 us)
Async XLA Ops:
  4.5 109.3 %copy-start = (bf16[64,8,512]{2,1,0:T(8,128)(2,1)S(1)}, bf16[64,8,512]{2,1,0:T(8,128)(2,1)}, u32[]{:S(2)}) copy-start(bf16[64,8,512]{2,1,0:T(8,128)(2,1)} %param.7) | copy-start | bytes 1572868
  113.9 43.4 %collective-permute-start.5 = (bf16[64,8,512]{2,0,1:T(8,128)(2,1)S(1)}, bf16[64,8,512]{2,0,1:T(8,128)(2,1)S(1)}, u32[]{:S(2)}, u32[]{:S(2)}) collective-permute-start(bf16[64,8,512]{2,0,1:T(8,128)(2,1)S(1)} %copy.10), channel_id=1, source_target_pairs={{0,128},{64,192},{128,0},{192,64},{1,129},{65,193},{129,1},{193,65... | collective-permute-start | bytes 1572872 | tf_op jit(solution)/shard_map/ppermute | solution.py:283
  122.3 13.7 %collective-permute-start.1 = (bf16[2,272,128]{2,1,0:T(8,128)(2,1)S(1)}, bf16[2,272,128]{2,1,0:T(8,128)(2,1)S(1)}, u32[]{:S(2)}, u32[]{:S(2)}) collective-permute-start(bf16[2,272,128]{2,1,0:T(8,128)(2,1)S(1)} %get-tuple-element.22), channel_id=1, source_target_pairs={{0,0},{2,64},{4,128},{6,192},{64,2},{66,66},{68,130},{70,194},{128... | collective-permute-start | bytes 417800 | tf_op jit(solution)/shard_map/ppermute | solution.py:288
  122.9 28.5 %collective-permute-start.2 = (bf16[2,272,128]{2,1,0:T(8,128)(2,1)S(1)}, bf16[2,272,128]{2,1,0:T(8,128)(2,1)S(1)}, u32[]{:S(2)}, u32[]{:S(2)}) collective-permute-start(bf16[2,272,128]{2,1,0:T(8,128)(2,1)S(1)} %get-tuple-element.23), channel_id=1, source_target_pairs={{0,64},{2,128},{4,192},{6,0},{64,66},{66,130},{68,194},{70,2},{128... | collective-permute-start | bytes 417800 | tf_op jit(solution)/shard_map/ppermute | solution.py:288
  127.7 23.8 %collective-permute-start.3 = (bf16[2,272,128]{2,1,0:T(8,128)(2,1)S(1)}, bf16[2,272,128]{2,1,0:T(8,128)(2,1)S(1)}, u32[]{:S(2)}, u32[]{:S(2)}) collective-permute-start(bf16[2,272,128]{2,1,0:T(8,128)(2,1)S(1)} %get-tuple-element.24), channel_id=1, source_target_pairs={{0,128},{2,192},{4,0},{6,64},{64,130},{66,194},{68,2},{70,66},{128... | collective-permute-start | bytes 417800 | tf_op jit(solution)/shard_map/ppermute | solution.py:288
  136.0 15.5 %collective-permute-start.4 = (bf16[2,272,128]{2,1,0:T(8,128)(2,1)S(1)}, bf16[2,272,128]{2,1,0:T(8,128)(2,1)S(1)}, u32[]{:S(2)}, u32[]{:S(2)}) collective-permute-start(bf16[2,272,128]{2,1,0:T(8,128)(2,1)S(1)} %get-tuple-element.25), channel_id=1, source_target_pairs={{0,192},{2,0},{4,64},{6,128},{64,194},{66,2},{68,66},{70,130},{128... | collective-permute-start | bytes 417800 | tf_op jit(solution)/shard_map/ppermute | solution.py:288
  136.0 27.9 %collective-permute-start = (bf16[64,8,512]{2,0,1:T(8,128)(2,1)S(1)}, bf16[64,8,512]{2,0,1:T(8,128)(2,1)S(1)}, u32[]{:S(2)}, u32[]{:S(2)}) collective-permute-start(bf16[64,8,512]{2,0,1:T(8,128)(2,1)S(1)} %copy.10), channel_id=1, source_target_pairs={{0,64},{64,0},{128,192},{192,128},{1,65},{65,1},{129,193},{193,129... | collective-permute-start | bytes 1572872 | tf_op jit(solution)/shard_map/ppermute | solution.py:283
  157.3 6.6 %collective-permute-start.6 = (bf16[64,8,512]{2,0,1:T(8,128)(2,1)S(1)}, bf16[64,8,512]{2,0,1:T(8,128)(2,1)S(1)}, u32[]{:S(2)}, u32[]{:S(2)}) collective-permute-start(bf16[64,8,512]{2,0,1:T(8,128)(2,1)S(1)} %collective-permute-done.5), channel_id=1, source_target_pairs={{0,64},{64,0},{128,192},{192,128},{1,65},{65,1},{129,193},{193,129... | collective-permute-start | bytes 1572872 | tf_op jit(solution)/shard_map/ppermute | solution.py:283
  158.7 6.0 %collective-permute-start.7 = (bf16[2,64,256]{2,1,0:T(8,128)(2,1)S(1)}, bf16[2,64,256]{2,1,0:T(8,128)(2,1)S(1)}, u32[]{:S(2)}, u32[]{:S(2)}) collective-permute-start(bf16[2,64,256]{2,1,0:T(8,128)(2,1)S(1)} %get-tuple-element.32), channel_id=1, source_target_pairs={{0,64},{64,0},{128,192},{192,128},{1,65},{65,1},{129,193},{193,129... | collective-permute-start | bytes 196616 | tf_op jit(solution)/shard_map/ppermute | solution.py:283
  158.8 7.4 %collective-permute-start.8 = (bf16[2,64,256]{2,1,0:T(8,128)(2,1)S(1)}, bf16[2,64,256]{2,1,0:T(8,128)(2,1)S(1)}, u32[]{:S(2)}, u32[]{:S(2)}) collective-permute-start(bf16[2,64,256]{2,1,0:T(8,128)(2,1)S(1)} %get-tuple-element.33), channel_id=1, source_target_pairs={{0,128},{64,192},{128,0},{192,64},{1,129},{65,193},{129,1},{193,65... | collective-permute-start | bytes 196616 | tf_op jit(solution)/shard_map/ppermute | solution.py:283
  163.9 5.9 %collective-permute-start.9 = (bf16[2,64,256]{2,1,0:T(8,128)(2,1)S(1)}, bf16[2,64,256]{2,1,0:T(8,128)(2,1)S(1)}, u32[]{:S(2)}, u32[]{:S(2)}) collective-permute-start(bf16[2,64,256]{2,1,0:T(8,128)(2,1)S(1)} %get-tuple-element.34), channel_id=1, source_target_pairs={{0,192},{64,128},{128,64},{192,0},{1,193},{65,129},{129,65},{193,1... | collective-permute-start | bytes 196616 | tf_op jit(solution)/shard_map/ppermute | solution.py:283

commit v4 on v2

--- a/solution.py
+++ b/solution.py
@@ -22,6 +22,7 @@
 PACK = 2 * HALF + 16
 GROUP = ("mem", "ylo", "x", "zp")
 STEP = 8
+ALONG = (0, 2, 1, 3)
 TAGS = 16
 
 
@@ -32,6 +33,7 @@
     blocks = anom_ref.shape[0]
     regions = out_ref.shape[0]
     zq_ways, plane_ways, zp_ways = ways
+    zq = lax.axis_index("zq")
 
     def load(g):
         part = pl.ds(g * STEP, STEP)
@@ -60,7 +62,9 @@
             rank = counts[region]
             counts[region] = rank + 1
             rest = region // zp_ways
-            place = (rest % zq_ways * plane_ways + rest // zq_ways) * zp_ways + region % zp_ways
+            along = (rest % zq_ways - zq + zq_ways) % zq_ways
+            mem = along % 2 * 2 + along // 2
+            place = (mem * plane_ways + rest // zq_ways) * zp_ways + region % zp_ways
 
             weight = jnp.where(row < tally_smem[b], spread_t[:, j : j + 1], 0.0)
             scaled = anom_buf[b].astype(jnp.float32) * weight
@@ -104,7 +108,7 @@
 
 def gram_kernel(tag_ref, rows_ref, *refs):
     outs, (upper, corner, tag_vmem, tag_smem, tag_sem) = refs[:4], refs[4:]
-    step, zq = pl.program_id(0), lax.axis_index("zq")
+    step, mem = pl.program_id(0), lax.axis_index("mem")
     sources = rows_ref.shape[0]
 
     @pl.when(step == 0)
@@ -125,7 +129,7 @@
         for i in range(CAP):
             code = tag_smem[step * sources + s, 0]
             tag = (code // TAGS if i else code % TAGS) - 1
-            turned = (tag // 2 - zq + 4) % 4 * 2 + tag % 2
+            turned = ((tag // 2) ^ mem) * 2 + tag % 2
             tag = jnp.where(tag >= 0, turned, PATCH_REG)
             block = rows_ref[s, i * OB : (i + 1) * OB, :]
             flipped = block.T
@@ -284,7 +288,7 @@
 
 
 def to_owner(x, e):
-    pairs = [(m * 4 + z, (z + e) % 4 * 4 + m) for m in range(4) for z in range(4)]
+    pairs = [(m * 4 + z, (m ^ e) * 4 + (z + ALONG[m]) % 4) for m in range(4) for z in range(4)]
     return lax.ppermute(x, ("mem", "zq"), pairs)
 
 
@@ -297,15 +301,17 @@
     )
     arrived = lax.all_to_all(messages, GROUP, split_axis=0, concat_axis=0, tiled=True)
 
+    arrived, prior = lax.optimization_barrier((arrived, prior))
+    near, far = swap(prior, 1), swap(prior, 2)
+
     pieces = partial_grams(arrived)
-    pieces, prior = lax.optimization_barrier((pieces, prior))
     pieces = [to_owner(pieces[e], e) for e in range(4)]
 
-    near, far = swap(prior, 1), swap(prior, 2)
     farther = swap(far, 1)
     field = jnp.concatenate([prior, near, far, farther], axis=0).transpose(1, 0, 2)
     state_mean = jnp.sum(field, axis=1, keepdims=True, dtype=jnp.float32) / SAMPLE_NUMBER
     perturb = (field - state_mean).astype(jnp.bfloat16)
+    pieces, state_mean, perturb = lax.optimization_barrier((pieces, state_mean, perturb))
 
     weights = flipped_weights(pieces)
     routed = [weights[0]] + [swap(weights[e], e) for e in range(1, 4)]

time: 190 us -> 178 us (0.937)
  starting transfers between devices: 33.5 us -> 19.1 us
  waiting for transfers between devices: 23.3 us -> 25.6 us
    ppermute x4, starting transfers between devices: 28.6 us -> 11.5 us  [to_owner(): return lax.ppermute(x, ('mem', 'zq'), pairs)]
    ppermute x4, waiting for transfers between devices: 4.05 us -> 6.99 us  [to_owner(): return lax.ppermute(x, ('mem', 'zq'), pairs)]
    ppermute x6, starting transfers between devices: 4.85 us -> 7.58 us  [swap(): return lax.ppermute(x, 'mem', [(j, j ^ bit) for j in range(4)])]
  transfers between devices with their start and end apart: 10 -> 10, of which waited for: 5 -> 5; matrix products, arithmetic and copies ran while one was open for 0% -> 0% of each run, Pallas kernels for 3% -> 4%
where the time goes in v4:
time: 178 us; the launch traced here: 175 us
  blocking collectives  109 us (61%)
  waiting for transfers between devices  25.6 us (14%)
  starting transfers between devices  19.1 us (11%)
  Pallas kernels  18.8 us (11%)
    all_to_all x1, blocking collectives, per_device(): lax.all_to_all(messages, GROUP, split_axis=0, concat_axis=0, tiled=True)  109 us
    ppermute x6, waiting for transfers between devices, swap(): return lax.ppermute(x, 'mem', [(j, j ^ bit) for j in range(4)])  18.6 us
    ppermute x4, starting transfers between devices, to_owner(): return lax.ppermute(x, ('mem', 'zq'), pairs)  11.5 us
    ppermute x6, starting transfers between devices, swap(): return lax.ppermute(x, 'mem', [(j, j ^ bit) for j in range(4)])  7.58 us
    pallas_call x1, Pallas kernels, partial_grams(): pl.pallas_call(gram_kernel, out_shape=[piece] * 4, grid_spec=pl.GridSpec(...  7.44 us
    ppermute x4, waiting for transfers between devices, to_owner(): return lax.ppermute(x, ('mem', 'zq'), pairs)  6.99 us
    pallas_call x1, Pallas kernels, flipped_weights(): pl.pallas_call(newton_kernel, out_shape=[piece] * 4, scratch_shapes=[pltp...  5.84 us
    pallas_call x1, Pallas kernels, build_messages(): pl.pallas_call(functools.partial(prep_kernel, ways), out_shape=jax.ShapeD...  4.99 us
  transfers between devices with their start and end apart: 10, of which 5 were waited for; matrix products, arithmetic and copies ran while one was open for 0% of the time, Pallas kernels for 4%

profile of v4, /device:TPU:40, one launch (start us, length us, event | category | flops | bytes accessed | tf_op | source)
XLA Modules:
  0.0 174.8 jit_solution(5811298468088367628)
XLA Ops:
  0.0 5.0 %build_messages.1 = bf16[64,264,256]{2,1,0:T(8,128)(2,1)S(1)} custom-call(s32[64]{0:T(128)} %bitcast.8, s32[64]{0:T(128)} %tally_smem.1, s32[64]{0:T(128)} %tile_smem.1, bf16[64,128,256]{2,1,0:T(8,128)(2,1)} %anom_ref.1, f32[64,128]{1,0:T(8,128)} %spread_ref.1, f32[64,128]{1,0:T(8,128)} %depart_ref.1), custom_call_target="tpu_custom_call" | custom-call | bytes 8388608 | tf_op jit(solution)/shard_map/build_messages/pallas_call | solution.py:87
  5.0 0.0 copy-start
  5.0 109.3 %all_to_all.5.tag_ref.rows_ref = bf16[64,264,256]{2,1,0:T(8,128)(2,1)S(1)} all-to-all(bf16[64,264,256]{2,1,0:T(8,128)(2,1)S(1)} %build_messages.1), channel_id=1, replica_groups=mesh['mem'=4,'ylo'=2,'x'=4,'zq'=4,'zp'=2] {'mem','ylo','x','zp'}, dimensions={0} | all-to-all | bytes 17301504 | tf_op jit(solution)/shard_map/all_to_all | solution.py:302
  114.3 0.0 copy-done
  114.3 0.2 copy.10
  114.5 0.9 collective-permute-start.5
  115.4 0.0 collective-permute-start.4
  115.4 14.3 %collective-permute-done.5 = bf16[64,8,512]{2,0,1:T(8,128)(2,1)S(1)} collective-permute-done((bf16[64,8,512]{2,0,1:T(8,128)(2,1)S(1)}, bf16[64,8,512]{2,0,1:T(8,128)(2,1)S(1)}, u32[]{:S(2)}, u32[]{:S(2)}) %collective-permute-start.5) | collective-permute-done | bytes 524320 | tf_op jit(solution)/shard_map/ppermute | solution.py:287
  129.6 0.0 collective-permute-start.6
  129.6 7.4 %partial_grams.1 = (bf16[2,272,128]{2,1,0:T(8,128)(2,1)S(1)}, bf16[2,272,128]{2,1,0:T(8,128)(2,1)S(1)}, bf16[2,272,128]{2,1,0:T(8,128)(2,1)S(1)}, bf16[2,272,128]{2,1,0:T(8,128)(2,1)S(1)}) custom-call(bf16[64,264,256]{2,1,0:T(8,128)(2,1)S(1)} %all_to_all.5.tag_ref.rows_ref, bf16[64,264,256]{2,1,0:T(8,128)(2,1)S(1)} %all_to_all.5.tag_ref.rows_ref), custom_call_target="tpu_custom_call" | custom-call | flops 2147483648 | bytes 8388608 | tf_op jit(solution)/shard_map/partial_grams/pallas_call | solution.py:172
  137.1 0.7 collective-permute-start
  137.8 7.9 %collective-permute-start.1 = (bf16[2,272,128]{2,1,0:T(8,128)(2,1)S(1)}, bf16[2,272,128]{2,1,0:T(8,128)(2,1)S(1)}, u32[]{:S(2)}, u32[]{:S(2)}) collective-permute-start(bf16[2,272,128]{2,1,0:T(8,128)(2,1)S(1)} %get-tuple-element.23), channel_id=1, source_target_pairs={{0,64},{2,66},{4,68},{6,70},{64,4},{66,6},{68,0},{70,2},{128,194},... | collective-permute-start | bytes 417800 | tf_op jit(solution)/shard_map/ppermute | solution.py:292
  145.6 0.0 collective-permute-start.2
  145.6 0.0 collective-permute-done.4
  145.6 3.0 %collective-permute-start.3 = (bf16[2,272,128]{2,1,0:T(8,128)(2,1)S(1)}, bf16[2,272,128]{2,1,0:T(8,128)(2,1)S(1)}, u32[]{:S(2)}, u32[]{:S(2)}) collective-permute-start(bf16[2,272,128]{2,1,0:T(8,128)(2,1)S(1)} %get-tuple-element.25), channel_id=1, source_target_pairs={{0,192},{2,194},{4,196},{6,198},{64,132},{66,134},{68,128},{70,130... | collective-permute-start | bytes 417800 | tf_op jit(solution)/shard_map/ppermute | solution.py:292
  148.6 0.0 collective-permute-done.6
  148.6 0.3 bitcast_reduce_fusion
  148.9 0.4 fusion.perturb_ref
  149.4 0.0 collective-permute-done.a_ref
  149.4 3.4 %collective-permute-done.1.b_ref = bf16[2,272,128]{2,1,0:T(8,128)(2,1)S(1)} collective-permute-done((bf16[2,272,128]{2,1,0:T(8,128)(2,1)S(1)}, bf16[2,272,128]{2,1,0:T(8,128)(2,1)S(1)}, u32[]{:S(2)}, u32[]{:S(2)}) %collective-permute-start.1) | collective-permute-done | bytes 139296 | tf_op jit(solution)/shard_map/ppermute | solution.py:292
  152.7 3.6 %collective-permute-done.2.c_ref = bf16[2,272,128]{2,1,0:T(8,128)(2,1)S(1)} collective-permute-done((bf16[2,272,128]{2,1,0:T(8,128)(2,1)S(1)}, bf16[2,272,128]{2,1,0:T(8,128)(2,1)S(1)}, u32[]{:S(2)}, u32[]{:S(2)}) %collective-permute-start.2) | collective-permute-done | bytes 139296 | tf_op jit(solution)/shard_map/ppermute | solution.py:292
  156.4 0.0 collective-permute-done.3.d_ref
  156.4 5.8 %weights.1 = (bf16[2,64,256]{2,1,0:T(8,128)(2,1)S(1)}, bf16[2,64,256]{2,1,0:T(8,128)(2,1)S(1)}, bf16[2,64,256]{2,1,0:T(8,128)(2,1)S(1)}, bf16[2,64,256]{2,1,0:T(8,128)(2,1)S(1)}) custom-call(bf16[2,272,128]{2,1,0:T(8,128)(2,1)S(1)} %collective-permute-done.a_ref, bf16[2,272,128]{2,1,0:T(8,128)(2,1)S(1)} %collective-permute-done.1.b_ref, ...), custom_call_target="tpu_custom_call" | custom-call | tf_op jit(solution)/shard_map/weights/pallas_call | solution.py:253
  162.2 3.7 %collective-permute-start.7 = (bf16[2,64,256]{2,1,0:T(8,128)(2,1)S(1)}, bf16[2,64,256]{2,1,0:T(8,128)(2,1)S(1)}, u32[]{:S(2)}, u32[]{:S(2)}) collective-permute-start(bf16[2,64,256]{2,1,0:T(8,128)(2,1)S(1)} %get-tuple-element.34), channel_id=1, source_target_pairs={{0,64},{64,0},{128,192},{192,128},{1,65},{65,1},{129,193},{193,129... | collective-permute-start | bytes 196616 | tf_op jit(solution)/shard_map/ppermute | solution.py:287
  165.9 1.7 collective-permute-start.8
  167.7 1.2 collective-permute-start.9
  168.9 0.0 collective-permute-done.7.refs_1_
  168.9 2.8 %collective-permute-done.8.refs_2_ = bf16[2,64,256]{2,1,0:T(8,128)(2,1)S(1)} collective-permute-done((bf16[2,64,256]{2,1,0:T(8,128)(2,1)S(1)}, bf16[2,64,256]{2,1,0:T(8,128)(2,1)S(1)}, u32[]{:S(2)}, u32[]{:S(2)}) %collective-permute-start.8) | collective-permute-done | bytes 65568 | tf_op jit(solution)/shard_map/ppermute | solution.py:287
  171.7 1.5 collective-permute-done.9.refs_3_
  173.3 0.5 analysed.1
  173.7 1.1 copy.11
  (2 shorter events, 0.0 us)
Async XLA Ops:
  5.0 109.3 %copy-start = (bf16[64,8,512]{2,1,0:T(8,128)(2,1)S(1)}, bf16[64,8,512]{2,1,0:T(8,128)(2,1)}, u32[]{:S(2)}) copy-start(bf16[64,8,512]{2,1,0:T(8,128)(2,1)} %param.7) | copy-start | bytes 1572868
  114.5 15.2 %collective-permute-start.5 = (bf16[64,8,512]{2,0,1:T(8,128)(2,1)S(1)}, bf16[64,8,512]{2,0,1:T(8,128)(2,1)S(1)}, u32[]{:S(2)}, u32[]{:S(2)}) collective-permute-start(bf16[64,8,512]{2,0,1:T(8,128)(2,1)S(1)} %copy.10), channel_id=1, source_target_pairs={{0,128},{64,192},{128,0},{192,64},{1,129},{65,193},{129,1},{193,65... | collective-permute-start | bytes 1572872 | tf_op jit(solution)/shard_map/ppermute | solution.py:287
  115.4 30.3 %collective-permute-start.4 = (bf16[64,8,512]{2,0,1:T(8,128)(2,1)S(1)}, bf16[64,8,512]{2,0,1:T(8,128)(2,1)S(1)}, u32[]{:S(2)}, u32[]{:S(2)}) collective-permute-start(bf16[64,8,512]{2,0,1:T(8,128)(2,1)S(1)} %copy.10), channel_id=1, source_target_pairs={{0,64},{64,0},{128,192},{192,128},{1,65},{65,1},{129,193},{193,129... | collective-permute-start | bytes 1572872 | tf_op jit(solution)/shard_map/ppermute | solution.py:287
  129.6 19.0 %collective-permute-start.6 = (bf16[64,8,512]{2,0,1:T(8,128)(2,1)S(1)}, bf16[64,8,512]{2,0,1:T(8,128)(2,1)S(1)}, u32[]{:S(2)}, u32[]{:S(2)}) collective-permute-start(bf16[64,8,512]{2,0,1:T(8,128)(2,1)S(1)} %collective-permute-done.5), channel_id=1, source_target_pairs={{0,64},{64,0},{128,192},{192,128},{1,65},{65,1},{129,193},{193,129... | collective-permute-start | bytes 1572872 | tf_op jit(solution)/shard_map/ppermute | solution.py:287
  137.1 12.3 %collective-permute-start = (bf16[2,272,128]{2,1,0:T(8,128)(2,1)S(1)}, bf16[2,272,128]{2,1,0:T(8,128)(2,1)S(1)}, u32[]{:S(2)}, u32[]{:S(2)}) collective-permute-start(bf16[2,272,128]{2,1,0:T(8,128)(2,1)S(1)} %get-tuple-element.22), channel_id=1, source_target_pairs={{0,0},{2,2},{4,4},{6,6},{64,68},{66,70},{68,64},{70,66},{128,130},... | collective-permute-start | bytes 417800 | tf_op jit(solution)/shard_map/ppermute | solution.py:292
  137.8 15.0 %collective-permute-start.1 = (bf16[2,272,128]{2,1,0:T(8,128)(2,1)S(1)}, bf16[2,272,128]{2,1,0:T(8,128)(2,1)S(1)}, u32[]{:S(2)}, u32[]{:S(2)}) collective-permute-start(bf16[2,272,128]{2,1,0:T(8,128)(2,1)S(1)} %get-tuple-element.23), channel_id=1, source_target_pairs={{0,64},{2,66},{4,68},{6,70},{64,4},{66,6},{68,0},{70,2},{128,194},... | collective-permute-start | bytes 417800 | tf_op jit(solution)/shard_map/ppermute | solution.py:292
  145.6 10.8 %collective-permute-start.2 = (bf16[2,272,128]{2,1,0:T(8,128)(2,1)S(1)}, bf16[2,272,128]{2,1,0:T(8,128)(2,1)S(1)}, u32[]{:S(2)}, u32[]{:S(2)}) collective-permute-start(bf16[2,272,128]{2,1,0:T(8,128)(2,1)S(1)} %get-tuple-element.24), channel_id=1, source_target_pairs={{0,128},{2,130},{4,132},{6,134},{64,196},{66,198},{68,192},{70,194... | collective-permute-start | bytes 417800 | tf_op jit(solution)/shard_map/ppermute | solution.py:292
  145.6 10.8 %collective-permute-start.3 = (bf16[2,272,128]{2,1,0:T(8,128)(2,1)S(1)}, bf16[2,272,128]{2,1,0:T(8,128)(2,1)S(1)}, u32[]{:S(2)}, u32[]{:S(2)}) collective-permute-start(bf16[2,272,128]{2,1,0:T(8,128)(2,1)S(1)} %get-tuple-element.25), channel_id=1, source_target_pairs={{0,192},{2,194},{4,196},{6,198},{64,132},{66,134},{68,128},{70,130... | collective-permute-start | bytes 417800 | tf_op jit(solution)/shard_map/ppermute | solution.py:292
  162.2 6.7 %collective-permute-start.7 = (bf16[2,64,256]{2,1,0:T(8,128)(2,1)S(1)}, bf16[2,64,256]{2,1,0:T(8,128)(2,1)S(1)}, u32[]{:S(2)}, u32[]{:S(2)}) collective-permute-start(bf16[2,64,256]{2,1,0:T(8,128)(2,1)S(1)} %get-tuple-element.34), channel_id=1, source_target_pairs={{0,64},{64,0},{128,192},{192,128},{1,65},{65,1},{129,193},{193,129... | collective-permute-start | bytes 196616 | tf_op jit(solution)/shard_map/ppermute | solution.py:287
  165.9 5.8 %collective-permute-start.8 = (bf16[2,64,256]{2,1,0:T(8,128)(2,1)S(1)}, bf16[2,64,256]{2,1,0:T(8,128)(2,1)S(1)}, u32[]{:S(2)}, u32[]{:S(2)}) collective-permute-start(bf16[2,64,256]{2,1,0:T(8,128)(2,1)S(1)} %get-tuple-element.35), channel_id=1, source_target_pairs={{0,128},{64,192},{128,0},{192,64},{1,129},{65,193},{129,1},{193,65... | collective-permute-start | bytes 196616 | tf_op jit(solution)/shard_map/ppermute | solution.py:287
  167.7 5.6 %collective-permute-start.9 = (bf16[2,64,256]{2,1,0:T(8,128)(2,1)S(1)}, bf16[2,64,256]{2,1,0:T(8,128)(2,1)S(1)}, u32[]{:S(2)}, u32[]{:S(2)}) collective-permute-start(bf16[2,64,256]{2,1,0:T(8,128)(2,1)S(1)} %get-tuple-element.36), channel_id=1, source_target_pairs={{0,192},{64,128},{128,64},{192,0},{1,193},{65,129},{129,65},{193,1... | collective-permute-start | bytes 196616 | tf_op jit(solution)/shard_map/ppermute | solution.py:287
